TPU v7x, 128 devices: a whole 4x4x4 slice. The times are simulated.
128 devices in a mesh: grp: 8 (over y, x_lo), cell: 16 (over x_hi, z, core).
Axes of the slice: x: 4 (x_hi: 2, x_lo: 2; x = x_hi * 2 + x_lo), y: 4, z: 4, core: 2. Of those that a mesh axis runs over, the one named last changes fastest.
Arguments:
- expression: bfloat16 [2000, 65536], P(None, ('grp', 'cell')), may hold values from 0.019897461 to 4
- dataset_id: int32 [65536], P(('grp', 'cell')), may hold values from 0 to 7, as said below
- dataset_map: int32 [8], P('grp'), may hold values from 0 to 7, as said below
- sweep_count: int32 [8], replicated, may hold values from 2 to 4
- picks: int32 [2, 16384], P(None, ('grp', 'cell')), may hold values from 0 to 511
- shared_init: float32 [64, 2000], replicated, may hold values from 0.004 to 0.06
- specific_init: float32 [8, 64, 2000], P('grp'), may hold values from 0.001 to 0.02
Outputs:
- loadings: float32 [2, 64, 16384], P(None, None, ('grp', 'cell'))
- shared_basis: float32 [64, 2000], replicated
- specific_basis: float32 [8, 64, 2000], P('grp')
Inputs may be any that keep to these rules, and one draw needn't show every extreme that they name: `dataset_map`: a permutation of the datasets; entry g is the one dataset of device group g. `dataset_id`: every cell held by the devices of group g belongs to one of the datasets that dataset_map gives to group g. `picks`: an index into the cells held by the device that holds the slot; a cell may be picked more than once.
All inputs are finite; a program needn't handle non-finite values.
Results may differ from a plain program's by a relative error of at most 0.0065.
The roundings to bfloat16 on the way count: a program that leaves them out, or rounds other values in their place, can miss the bound.
Values sent between devices are 32-bit elements; how exact they have to be, the bound alone decides.
No kernel may reach another device: no remote copies, remote signals or barrier semaphores. Data moves between devices by JAX's collectives and lax.ppermute only.
A program may use at most 128 MiB of HBM per device.

v0:
```python
import jax
import jax.numpy as jnp
from jax import lax
from jax.sharding import PartitionSpec as P

K = 64
SWEEPS = 4


EPSILON = 1e-06
LAMBDA = 5.0
HIGHEST = lax.Precision.HIGHEST


def hals_loadings(target, gram_matrix, member, counts):
    divisor = jnp.einsum(
        "jk,jn->kn",
        jnp.diagonal(gram_matrix, axis1=1, axis2=2) + EPSILON,
        member,
        precision=HIGHEST,
    )

    def sweep(sweep_index, current):
        active = sweep_index < counts
        for factor in range(K):
            row_terms = jnp.einsum(
                "jl,ln->jn", gram_matrix[:, factor, :], current, precision=HIGHEST
            )
            product = jnp.sum(row_terms * member, axis=0)
            updated = jnp.maximum(
                current[factor] + (target[factor] - product) / divisor[factor], 0.0
            )
            current = current.at[factor].set(jnp.where(active, updated, current[factor]))
        return current

    return lax.fori_loop(0, SWEEPS, sweep, jnp.zeros(target.shape, jnp.float32))


def solve_loadings(cell_data, member, counts, shared, specific):
    combined = shared[None] + specific
    slot_total = specific.shape[0]
    stacked = combined.astype(jnp.bfloat16).reshape(slot_total * K, combined.shape[2])
    target = jnp.dot(stacked, cell_data, preferred_element_type=jnp.float32)
    target = jnp.sum(target.reshape(slot_total, K, cell_data.shape[1]) * member[:, None, :], axis=0)
    gram_matrix = jnp.einsum(
        "jkg,jlg->jkl", combined, combined, precision=HIGHEST
    ) + LAMBDA * jnp.einsum("jkg,jlg->jkl", specific, specific, precision=HIGHEST)
    return hals_loadings(target, gram_matrix, member, counts)


def renew_shared(shared, gram_total, carried):
    for factor in range(K):
        change = (
            carried[factor] - jnp.dot(gram_total[factor], shared, precision=HIGHEST)
        ) / jnp.maximum(gram_total[factor, factor], 1.0)
        shared = shared.at[factor].set(jnp.maximum(shared[factor] + change, 0.0))
    return shared


def renew_specific(specific, shared, gram_sets, stat_sets):
    for factor in range(K):
        weights = gram_sets[:, factor, :]
        pulled = jnp.dot(weights, shared, precision=HIGHEST) + (1.0 + LAMBDA) * jnp.einsum(
            "sl,slg->sg", weights, specific, precision=HIGHEST
        )
        divisor = jnp.maximum((1.0 + LAMBDA) * gram_sets[:, factor, factor], 1.0)
        updated = jnp.maximum(
            specific[:, factor] + (stat_sets[:, factor] - pulled) / divisor[:, None], 0.0
        )
        specific = specific.at[:, factor].set(updated)
    return specific


def on_device(expression, dataset_id, dataset_map, sweep_count, picks, shared_init, specific_init):
    slot_total = dataset_map.shape[0]
    gene_count = expression.shape[0]
    listing = jnp.arange(sweep_count.shape[0], dtype=jnp.int32)
    slot_sweeps = jnp.sum(
        jnp.where(dataset_map[:, None] == listing[None, :], sweep_count[None, :], 0), axis=1
    )
    belongs = dataset_id[None, :] == dataset_map[:, None]
    pool_sweeps = jnp.sum(jnp.where(belongs, slot_sweeps[:, None], 0), axis=0)
    pool_member = belongs.astype(jnp.float32)
    basis_list = [(shared_init, specific_init)]
    group_grams = jnp.zeros((slot_total, K, K), jnp.float32)
    group_stats = jnp.zeros((slot_total, K, gene_count), jnp.float32)
    gram_total = jnp.zeros((K, K), jnp.float32)
    results = []
    for round_index in range(picks.shape[0]):
        chosen = picks[round_index]
        cell_data = jnp.take(expression, chosen, axis=1)
        member = jnp.take(pool_member, chosen, axis=1)
        counts = jnp.take(pool_sweeps, chosen)
        shared_use, specific_use = basis_list[max(round_index - 1, 0)]
        loadings = solve_loadings(cell_data, member, counts, shared_use, specific_use)
        results.append(loadings)
        masked = loadings.astype(jnp.bfloat16)[None] * member.astype(jnp.bfloat16)[:, None, :]
        stat_part = jnp.einsum("jkn,gn->jkg", masked, cell_data, preferred_element_type=jnp.float32)
        gram_part = jnp.einsum(
            "jkn,ln->jkl", loadings[None] * member[:, None, :], loadings, precision=HIGHEST
        )
        shared_prev, specific_prev = basis_list[-1]
        gram_inc, stat_inc = lax.psum((gram_part, stat_part), "cell")
        group_grams = group_grams + gram_inc
        group_stats = group_stats + stat_inc
        group_term = jnp.sum(group_stats, axis=0) - jnp.einsum(
            "jkl,jlg->kg", group_grams, specific_prev, precision=HIGHEST
        )
        gram_sum, carried = lax.psum((jnp.sum(gram_inc, axis=0), group_term), "grp")
        gram_total = gram_total + gram_sum
        shared_next = renew_shared(shared_prev, gram_total, carried)
        specific_next = renew_specific(specific_prev, shared_next, group_grams, group_stats)
        basis_list.append((shared_next, specific_next))
    return (jnp.stack(results), basis_list[-1][0], basis_list[-1][1])


def solution(mesh):
    return jax.shard_map(
        on_device,
        mesh=mesh,
        in_specs=(
            P(None, ("grp", "cell")),
            P(("grp", "cell")),
            P("grp"),
            P(),
            P(None, ("grp", "cell")),
            P(),
            P("grp", None, None),
        ),
        out_specs=(P(None, None, ("grp", "cell")), P(), P("grp", None, None)),
        check_vma=False,
    )
```

profile of v0, /device:TPU:1, one launch (start us, length us, event | category | flops | bytes accessed | tf_op | source)
XLA Modules:
  0.0 765.9 jit_solution(10395594412957789312)
XLA Ops:
  7.2 1.0 copy.418
  8.3 1.0 copy.417
  12.0 1.3 gather_fusion.4
  13.3 1.3 gather_fusion.6
  14.5 1.3 gather_fusion.3
  15.8 1.3 gather_fusion.1
  17.1 2.9 copy.12
  20.0 1.7 gather_fusion.5
  21.7 1.7 gather_fusion.2
  24.1 0.8 gather_fusion
  25.0 1.4 convolution_multiply_fusion
  26.4 46.4 %while.417 = (s32[]{:T(128)}, f32[64,128]{1,0:T(8,128)S(1)}, s32[128]{0:T(128)S(1)}, f32[64,128]{1,0:T(8,128)S(1)}, f32[1,64,64]{2,1,0:T(8,128)S(1)}, /*index=5*...) while((s32[]{:T(128)}, f32[64,128]{1,0:T(8,128)S(1)}, ...), condition=%wide.region_4.8_spmd, body=%wide.region_3.7_spmd.sunk | while | flops 6340738 | bytes 2393561 | solution.py:36
  73.3 46.6 %while.416 = (s32[]{:T(128)}, f32[64,128]{1,0:T(8,128)S(1)}, s32[128]{0:T(128)S(1)}, f32[64,128]{1,0:T(8,128)S(1)}, f32[1,64,64]{2,1,0:T(8,128)S(1)}, /*index=5*...) while((s32[]{:T(128)}, f32[64,128]{1,0:T(8,128)S(1)}, ...), condition=%wide.region_2.0_spmd, body=%wide.region_1.5_spmd.sunk | while | flops 6340738 | bytes 2393561 | solution.py:36
  119.9 1.1 convolution_bitcast_fusion.129
  121.0 1.1 convolution_bitcast_fusion.128
  122.5 66.4 %all-reduce = (f32[1,64,64]{2,1,0:T(8,128)S(1)}, f32[1,64,64]{2,1,0:T(8,128)S(1)}) all-reduce(f32[1,64,64]{2,1,0:T(8,128)S(1)} %convolution_bitcast_fusion.131, f32[1,64,64]{2,1,0:T(8,128)S(1)} %convolution_bitcast_fusion.130), channel_id=1, replica_groups=mesh['grp'=8,'cell'=16] {'cell'}, use_global_device_ids=true, to_apply=%region_6.10 | all-reduce | flops 8192 | bytes 65536 | tf_op jit(solution)/shard_map/psum | solution.py:103
  188.9 27.8 %all-reduce.2 = (f32[64,64]{1,0:T(8,128)S(1)}, f32[64,64]{1,0:T(8,128)S(1)}) all-reduce(f32[64,64]{1,0:T(8,128)S(1)} %bitcast.9809, f32[64,64]{1,0:T(8,128)S(1)} %bitcast.9810), channel_id=1, replica_groups=mesh['grp'=8,'cell'=16] {'grp'}, use_global_device_ids=true, to_apply=%region_8.12 | all-reduce | flops 8192 | bytes 65536 | tf_op jit(solution)/shard_map/psum | solution.py:109
  220.2 0.7 fusion.1721
  224.4 0.7 fusion.1716
  225.1 0.7 fusion.1715
  350.5 0.7 fusion.1713
  363.0 0.7 fusion.1712
  375.6 0.7 fusion.1711
  390.2 2.5 convolution_subtract_fusion.1
  392.7 1.9 fusion.1705
  394.6 1.8 fusion.1704
  397.1 78.0 %all-reduce.7.cloned.1.call-done = f32[64,2000]{1,0:T(8,128)} async-done(((f32[64,2000]{1,0:T(8,128)}), f32[64,2000]{1,0:T(8,128)}) %all-reduce.7.cloned.1.call-update) | async-done | bytes 512016 | tf_op jit(solution)/shard_map/psum | solution.py:109
  475.1 1.4 fusion.1710
  578.4 1.4 convolution_subtract_fusion
  580.6 74.6 %all-reduce.9.cloned.1.call-done = f32[64,2000]{1,0:T(8,128)} async-done(((f32[64,2000]{1,0:T(8,128)}), f32[64,2000]{1,0:T(8,128)}) %all-reduce.9.cloned.1.call-update) | async-done | bytes 512016 | tf_op jit(solution)/shard_map/psum | solution.py:109
  655.2 1.5 fusion.1702
  758.4 0.8 copy-done.3
  (2265 shorter events, 304.5 us)
Async XLA Ops:
  7.2 3.5 copy-start.10
  7.2 3.5 copy-start.12
  7.2 3.5 copy-start.11
  7.2 383.0 %all-reduce.11.cloned.1.call-start = ((), (), s32[]{:S(2)}) async-start(), calls=%async_computation.2 | async-start | bytes 2097152 | tf_op jit(solution)/shard_map/psum | solution.py:103
  9.3 380.1 %copy-start = (f32[64,2000]{1,0:T(8,128)}, f32[64,2000]{1,0:T(8,128)S(1)}, u32[]{:S(2)}) copy-start(f32[64,2000]{1,0:T(8,128)S(1)} %copy.417) | copy-start | bytes 1536004
  26.4 46.5 %copy-start.6 = (bf16[128,2000]{1,0:T(8,128)(2,1)S(1)}, bf16[128,2000]{1,0:T(8,128)(2,1)}, u32[]{:S(2)}) copy-start(bf16[128,2000]{1,0:T(8,128)(2,1)} %gather_fusion.2) | copy-start | bytes 1536004
  73.2 47.7 %copy-start.5 = (bf16[128,2000]{1,0:T(8,128)(2,1)S(1)}, bf16[128,2000]{1,0:T(8,128)(2,1)}, u32[]{:S(2)}) copy-start(bf16[128,2000]{1,0:T(8,128)(2,1)} %gather_fusion.5) | copy-start | bytes 1536004
  122.1 353.0 %all-reduce.7.cloned.1.call-start = ((), (), s32[]{:S(2)}) async-start(), calls=%async_computation | async-start | bytes 1048576 | tf_op jit(solution)/shard_map/psum | solution.py:109
  390.2 6.3 copy-start.4
  390.2 6.4 copy-start.7
  392.7 83.9 %slice-start = ((f32[64,2000]{1,0:T(8,128)}), f32[1,2000]{1,0:T(1,128)S(1)}, s32[]{:S(2)}) async-start(f32[64,2000]{1,0:T(8,128)} %copy-done), calls=%async_computation.3 | async-start | bytes 16384 | tf_op jit(solution)/shard_map/slice | solution.py:56
  392.7 83.9 %copy-start.1 = (f32[64,2000]{1,0:T(8,128)S(1)}, f32[64,2000]{1,0:T(8,128)}, u32[]{:S(2)}) copy-start(f32[64,2000]{1,0:T(8,128)} %copy-done) | copy-start | bytes 1536004
  396.9 258.4 %all-reduce.9.cloned.1.call-start = ((), (), s32[]{:S(2)}) async-start(), calls=%async_computation.1 | async-start | bytes 1048576 | tf_op jit(solution)/shard_map/psum | solution.py:109
  476.8 4.2 copy-start.8
  656.9 4.0 copy-start.9
  696.1 61.1 %copy-start.2 = (f32[64,2000]{1,0:T(8,128)}, f32[64,2000]{1,0:T(8,128)S(1)}, u32[]{:S(2)}) copy-start(f32[64,2000]{1,0:T(8,128)S(1)} %scatter.1727) | copy-start | bytes 1536004
  758.4 0.8 copy-start.3
Sparse Core Ops, SparseCore 0:
  122.2 144.8 all-reduce.10
  397.0 78.0 all-reduce.6
  579.9 75.2 all-reduce.8
where the time goes:
time: 780 us; the launch traced here: 766 us
  matrix products  227 us (29%)
  between operations  180 us (23%)
  waiting for transfers between devices  153 us (20%)
  local copies, waits for them, and re-layouts  106 us (14%)
  blocking collectives  94.2 us (12%)
    psum x2, waiting for transfers between devices, on_device(): gram_sum, carried = lax.psum((jnp.sum(gram_inc, axis=0), group_term), 'grp')  153 us
    dot_general x512, matrix products, sweep(): jnp.einsum('jl,ln->jn', gram_matrix[:, factor, :], current, precision=HIG...  78.7 us
    psum x1, blocking collectives, on_device(): gram_inc, stat_inc = lax.psum((gram_part, stat_part), 'cell')  66.4 us
    dot_general x128, matrix products, renew_shared(): jnp.dot(gram_total[factor], shared, precision=HIGHEST)  46.6 us
    dot_general x128, matrix products, renew_specific(): jnp.einsum('sl,slg->sg', weights, specific, precision=HIGHEST)  46.5 us
    dot_general x128, matrix products, renew_specific(): jnp.dot(weights, shared, precision=HIGHEST)  46.4 us
    psum x1, blocking collectives, on_device(): gram_sum, carried = lax.psum((jnp.sum(gram_inc, axis=0), group_term), 'grp')  27.8 us
    scatter x128, local copies, waits for them, and re-layouts, renew_specific(): specific = specific.at[:, factor].set(updated)  27.8 us
  transfers between devices with their start and end apart: 3, of which 2 were waited for; matrix products, arithmetic and copies ran while one was open for 2% of the time, Pallas kernels for 0%

commit v1 on v0

v1 whole, which is shorter than its diff:
```python
import jax
import jax.numpy as jnp
from jax import lax
from jax.experimental import pallas as pl
from jax.experimental.pallas import tpu as pltpu
from jax.sharding import Mesh, PartitionSpec as P

K = 64
G = 2000
N = 128
HALF = 8 * N
LAST = G - 15 * N
EPSILON = 1e-06
LAMBDA = 5.0
RIDGE = 1.0 + LAMBDA
HIGHEST = lax.Precision.HIGHEST
GRP = ("y", "xl")
RING = ("xh", "z")
ALL = ("y", "xl", "xh", "z", "c")
NT = (((1,), (1,)), ((), ()))
F32 = jnp.float32
BF16 = jnp.bfloat16


def dot_nt(a, b, precision=None):
    return lax.dot_general(a, b, NT, precision=precision, preferred_element_type=F32)


def diagonal(square):
    n = square.shape[0]
    rows = lax.broadcasted_iota(jnp.int32, (n, n), 0)
    cols = lax.broadcasted_iota(jnp.int32, (n, n), 1)
    return jnp.sum(jnp.where(rows == cols, square, 0.0), axis=1, keepdims=True)


def rows_of(x):
    return [x[8 * t : 8 * t + 8] for t in range(K // 8)]


def coordinate_steps(state, residual, column):
    sub = lax.broadcasted_iota(jnp.int32, (8, N), 0)
    for k in range(K):
        t, s = divmod(k, 8)
        cols = column(k)
        for half in range(len(state)):
            h, r = state[half], residual[half]
            change = jnp.maximum(-h[t], r[t])
            spread = jnp.broadcast_to(change[s : s + 1], (8, N))
            h[t] = jnp.where(sub == s, h[t] + change, h[t])
            for j in range(K // 8):
                r[j] = r[j] - cols[j] * spread
    return state


def front_kernel(where, dmap, sweeps, x, picks, w, v, loads, keep, send, w_own, v_own, table):
    core, tile = where[0], where[1]
    count = sweeps[dmap[0]]
    shared, specific = w[...], v[0]
    mixed = shared + specific

    @pl.when(tile < 15)
    def _():
        at = pl.multiple_of(jnp.minimum(tile, 14) * N, N)
        w_own[...] = w[:, pl.ds(at, N)]
        v_own[...] = v[0, :, pl.ds(at, N)]

    @pl.when(tile == 15)
    def _():
        w_own[...] = jnp.zeros((K, N), F32)
        v_own[...] = jnp.zeros((K, N), F32)
        w_own[:, :LAST] = w[:, 15 * N :]
        v_own[:, :LAST] = v[0, :, 15 * N :]

    gram = dot_nt(mixed, mixed, HIGHEST) + LAMBDA * dot_nt(specific, specific, HIGHEST)
    inverse = 1.0 / (diagonal(gram) + EPSILON)
    scaled = gram * inverse
    for k in range(K):
        table[k] = jnp.broadcast_to(scaled[:, k : k + 1], (K, N))

    pool = lax.broadcasted_iota(jnp.int32, (x.shape[1], N), 0)
    choose = jnp.concatenate(
        [(pool == picks[r : r + 1, :]).astype(F32).astype(BF16) for r in range(2)], axis=1
    )
    cells = jnp.dot(x[...], choose, preferred_element_type=F32).astype(BF16)
    target = jnp.dot(mixed.astype(BF16), cells, preferred_element_type=F32) * inverse

    def sweep(_, carry):
        state = [list(carry[0]), list(carry[1])]
        residual = [list(carry[2]), list(carry[3])]
        coordinate_steps(state, residual, lambda k: [table[k, 8 * j : 8 * j + 8] for j in range(K // 8)])
        return (tuple(state[0]), tuple(state[1]), tuple(residual[0]), tuple(residual[1]))

    none = tuple(jnp.zeros((8, N), F32) for _ in range(K // 8))
    carry = (none, none, tuple(rows_of(target[:, :N])), tuple(rows_of(target[:, N:])))
    carry = lax.fori_loop(0, count, sweep, carry)
    first = jnp.concatenate(carry[0], axis=0)
    second = jnp.concatenate(carry[1], axis=0)
    loads[0] = first
    loads[1] = second
    zero = jnp.zeros((K, N), F32)
    both = jnp.concatenate([first, second], axis=1)
    block = jnp.concatenate(
        [jnp.concatenate([first, zero], axis=1), jnp.concatenate([zero, second], axis=1)], axis=0
    )
    gram_part = dot_nt(both, block, HIGHEST)
    keep[HALF:] = gram_part
    send[HALF:] = gram_part
    rounded = block.astype(BF16)
    low = dot_nt(cells[:HALF], rounded)
    high = dot_nt(cells[HALF:], rounded)

    @pl.when(core == 0)
    def _():
        keep[:HALF] = low
        send[: G - HALF] = high
        send[G - HALF : HALF] = jnp.zeros((2 * HALF - G, N), F32)

    @pl.when(core == 1)
    def _():
        send[:HALF] = low
        keep[: G - HALF] = high
        keep[G - HALF : HALF] = jnp.zeros((2 * HALF - G, N), F32)


def pack_kernel(keep, came, out):
    gram = keep[HALF:] + came[HALF:]
    for i in range(8):
        out[i, :N] = keep[N * i : N * i + N] + came[N * i : N * i + N]
        out[i, N:] = gram


def group_kernel(came, v_own, out, stats, grams):
    total = came[0]
    for i in range(1, 8):
        total = total + came[i]
    rows = total[:N].T
    first = rows[:K]
    stats[0] = first
    stats[1] = first + rows[K:]
    gram = total[N:]
    grams[0] = gram[:, :K]
    grams[1] = gram[:, :K] + gram[:, K:]
    carried = first - jnp.dot(gram[:, :K], v_own[...], precision=HIGHEST, preferred_element_type=F32)
    for i in range(8):
        out[i, :K] = carried
        out[i, K:] = gram


def renew(w, v, gram_total, gram, carried, stat):
    inverse = 1.0 / jnp.maximum(diagonal(gram_total), 1.0)
    scaled = gram_total * inverse
    start = carried - jnp.dot(gram_total, w, precision=HIGHEST, preferred_element_type=F32)
    state, residual = [rows_of(w)], [rows_of(start * inverse)]

    def columns(table):
        return lambda k: rows_of(jnp.broadcast_to(table[:, k : k + 1], (K, N)))

    coordinate_steps(state, residual, columns(scaled))
    w_next = jnp.concatenate(state[0], axis=0)
    own_inverse = 1.0 / jnp.maximum(RIDGE * diagonal(gram), 1.0)
    own_scaled = (RIDGE * gram) * own_inverse
    pulled = jnp.dot(gram, w_next + RIDGE * v, precision=HIGHEST, preferred_element_type=F32)
    state, residual = [rows_of(v)], [rows_of((stat - pulled) * own_inverse)]
    coordinate_steps(state, residual, columns(own_scaled))
    return w_next, jnp.concatenate(state[0], axis=0)


def first_kernel(came, stats, grams, w_own, v_own, out, w_next, v_next, gram_total):
    total = came[0]
    for i in range(1, 8):
        total = total + came[i]
    all_grams = total[K:]
    gram_total[...] = all_grams[:, :K] + all_grams[:, K:]
    shared, specific = renew(w_own[...], v_own[...], all_grams[:, :K], grams[0], total[:K], stats[0])
    w_next[...] = shared
    v_next[...] = specific
    carried = stats[1] - jnp.dot(grams[1], specific, precision=HIGHEST, preferred_element_type=F32)
    for i in range(8):
        out[i] = carried


def second_kernel(came, stats, grams, w_own, v_own, gram_total, out):
    total = came[0]
    for i in range(1, 8):
        total = total + came[i]
    shared, specific = renew(w_own[...], v_own[...], gram_total[...], grams[1], total, stats[1])
    for i in range(8):
        out[i, :K] = shared
        out[i, K:] = specific


def finish_kernel(where, mine, other, w, v):
    def write(first, second):
        for half, part in enumerate((first, second)):
            for i in range(8):
                at = (8 * half + i) * N
                wide = min(N, G - at)
                w[:, at : at + wide] = part[i, :K, :wide]
                v[0, :, at : at + wide] = part[i, K:, :wide]

    @pl.when(where[0] == 0)
    def _():
        write(mine, other)

    @pl.when(where[0] == 1)
    def _():
        write(other, mine)


def shape(*dims):
    return jax.ShapeDtypeStruct(dims, F32)


VM = pl.BlockSpec(memory_space=pltpu.VMEM)
SM = pl.BlockSpec(memory_space=pltpu.SMEM)
SWAP = [(0, 1), (1, 0)]


def on_device(expression, dataset_id, dataset_map, sweep_count, picks, shared_init, specific_init):
    core = lax.axis_index("c")
    tile = core * 8 + lax.axis_index("xh") * 4 + lax.axis_index("z")
    where = jnp.stack([core, tile]).astype(jnp.int32)
    loads, keep, send, w_own, v_own = pl.pallas_call(
        front_kernel,
        name="front",
        out_shape=(shape(2, K, N), shape(HALF + K, N), shape(HALF + K, N), shape(K, N), shape(K, N)),
        in_specs=[SM, SM, SM, VM, VM, VM, VM],
        out_specs=[VM] * 5,
        scratch_shapes=[pltpu.VMEM((K, K, N), F32)],
    )(where, dataset_map, sweep_count, expression, picks, shared_init, specific_init)
    came = lax.ppermute(send, "c", SWAP)
    packed = pl.pallas_call(
        pack_kernel, name="pack", out_shape=shape(8, N + K, N), in_specs=[VM, VM], out_specs=VM
    )(keep, came)
    came = lax.all_to_all(packed, RING, 0, 0, tiled=True)
    spread, stats, grams = pl.pallas_call(
        group_kernel,
        name="group",
        out_shape=(shape(8, N, N), shape(2, K, N), shape(2, K, K)),
        in_specs=[VM, VM],
        out_specs=[VM] * 3,
    )(came, v_own)
    came = lax.all_to_all(spread, GRP, 0, 0, tiled=True)
    spread, w_own, v_own, gram_total = pl.pallas_call(
        first_kernel,
        name="first",
        out_shape=(shape(8, K, N), shape(K, N), shape(K, N), shape(K, K)),
        in_specs=[VM] * 5,
        out_specs=[VM] * 4,
    )(came, stats, grams, w_own, v_own)
    came = lax.all_to_all(spread, GRP, 0, 0, tiled=True)
    spread = pl.pallas_call(
        second_kernel, name="second", out_shape=shape(8, N, N), in_specs=[VM] * 6, out_specs=VM
    )(came, stats, grams, w_own, v_own, gram_total)
    mine = lax.all_to_all(spread, RING, 0, 0, tiled=True)
    other = lax.ppermute(mine, "c", SWAP)
    shared, specific = pl.pallas_call(
        finish_kernel,
        name="finish",
        out_shape=(shape(K, G), shape(1, K, G)),
        in_specs=[SM, VM, VM],
        out_specs=[VM, VM],
    )(where, mine, other)
    return loads, shared, specific


def solution(mesh):
    fine = Mesh(mesh.devices.reshape(4, 2, 2, 4, 2), ALL)
    return jax.shard_map(
        on_device,
        mesh=fine,
        in_specs=(P(None, ALL), P(ALL), P(GRP), P(), P(None, ALL), P(), P(GRP, None, None)),
        out_specs=(P(None, None, ALL), P(), P(GRP, None, None)),
        check_vma=False,
    )
```

time: 780 us -> 91.1 us (0.12); the launches traced: 766 us -> 90.1 us
  matrix products: 227 us -> 0 us
  between operations: 180 us -> 1.29 us
  waiting for transfers between devices: 153 us -> 3.33 us
  local copies, waits for them, and re-layouts: 106 us -> 1.62 us
  blocking collectives: 94.2 us -> 56.7 us
  Pallas kernels: 0 us -> 20.6 us
    dot_general x906 -> x0, matrix products: 227 us -> none  [the longest x512 78.7 us: sweep(): jnp.einsum('jl,ln->jn', gram_matrix[:, factor, :], current, precision=HIG...]
    psum x3 -> x0, waiting for transfers between devices: 153 us -> none  [the longest x2 153 us: on_device(): gram_sum, carried = lax.psum((jnp.sum(gram_inc, axis=0), group_term), 'grp')]
    psum x2 -> x0, blocking collectives: 94.2 us -> none  [the longest x1 66.4 us: on_device(): gram_inc, stat_inc = lax.psum((gram_part, stat_part), 'cell')]
    scatter x768 -> x0, local copies, waits for them, and re-layouts: 68 us -> none  [the longest x128 27.8 us: renew_specific(): specific = specific.at[:, factor].set(updated)]
    all_to_all x0 -> x4, blocking collectives: none -> 56.7 us  [the longest x2 21.8 us: on_device(): came = lax.all_to_all(spread, GRP, 0, 0, tiled=True)]
    slice x291 -> x0, local copies, waits for them, and re-layouts: 22.8 us -> none  [the longest x10 6.93 us: renew_specific(): divisor = jnp.maximum((1.0 + LAMBDA) * gram_sets[:, factor, factor], 1.0)]
    pallas_call x0 -> x6, Pallas kernels: none -> 20.6 us  [the longest x1 7.91 us: on_device(): pl.pallas_call(front_kernel, name='front', out_shape=(shape(2, K, N), sha...]
    gather x7 -> x0, local copies, waits for them, and re-layouts: 9.32 us -> none  [the longest x2 3.45 us: on_device(): cell_data = jnp.take(expression, chosen, axis=1)]
  transfers between devices with their start and end apart: 3 -> 2, of which waited for: 2 -> 2; matrix products, arithmetic and copies ran while one was open for 2% -> 0% of each run, Pallas kernels for 0% -> 0%
where the time goes in v1:
time: 91.1 us; the launch traced here: 90.1 us
  blocking collectives  56.7 us (62%)
  Pallas kernels  20.6 us (23%)
  starting transfers between devices  5.94 us (7%)
  waiting for transfers between devices  3.33 us (4%)
  local copies, waits for them, and re-layouts  1.62 us (2%)
  between operations  1.29 us (1%)
    all_to_all x2, blocking collectives, on_device(): came = lax.all_to_all(spread, GRP, 0, 0, tiled=True)  21.8 us
    all_to_all x1, blocking collectives, on_device(): came = lax.all_to_all(packed, RING, 0, 0, tiled=True)  20.5 us
    all_to_all x1, blocking collectives, on_device(): mine = lax.all_to_all(spread, RING, 0, 0, tiled=True)  14.4 us
    pallas_call x1, Pallas kernels, on_device(): pl.pallas_call(front_kernel, name='front', out_shape=(shape(2, K, N), sha...  7.91 us
    ppermute x1, starting transfers between devices, on_device(): other = lax.ppermute(mine, 'c', SWAP)  4.57 us
    pallas_call x1, Pallas kernels, on_device(): pl.pallas_call(first_kernel, name='first', out_shape=(shape(8, K, N), sha...  3.2 us
    pallas_call x1, Pallas kernels, on_device(): pl.pallas_call(second_kernel, name='second', out_shape=shape(8, N, N), in...  2.89 us
    pallas_call x1, Pallas kernels, on_device(): pl.pallas_call(finish_kernel, name='finish', out_shape=(shape(K, G), shap...  2.29 us
  transfers between devices with their start and end apart: 2, of which 2 were waited for; matrix products, arithmetic and copies ran while one was open for 0% of the time, Pallas kernels for 0%

profile of v1, /device:TPU:1, one launch (start us, length us, event | category | flops | bytes accessed | tf_op | source)
XLA Modules:
  0.0 90.1 jit_solution(8687220529987128165)
XLA Ops:
  1.3 0.6 pad_add_fusion.where
  1.9 7.9 %front.1 = (f32[2,64,128]{2,1,0:T(8,128)}, f32[1088,128]{1,0:T(8,128)}, f32[1088,128]{1,0:T(8,128)}, f32[64,128]{1,0:T(8,128)}, f32[64,128]{1,0:T(8,128)}) custom-call(s32[2]{0:T(128)} %pad_add_fusion.where, s32[1]{0:T(128)S(6)} %copy.9.dmap, s32[8]{0:T(128)} %sweeps.1, bf16[2000,512]{1,0:T(8,128)(2,1)} %x.1, s32[2,128]{1,0:T(2,128)} %picks.1, ...), custom_call_target="tpu_custom_call" | custom-call | tf_op jit(solution)/shard_map/front/pallas_call | solution.py:223
  9.8 1.4 %collective-permute-start = (f32[1088,128]{1,0:T(8,128)}, f32[1088,128]{1,0:T(8,128)S(1)}, u32[]{:S(2)}, u32[]{:S(2)}) collective-permute-start(f32[1088,128]{1,0:T(8,128)} %get-tuple-element.19), channel_id=1, source_target_pairs={{0,1},{1,0},{2,3},{3,2},{4,5},{5,4},{6,7},{7,6},{8,9},{9,8},{10,11... | collective-permute-start | bytes 1671176 | tf_op jit(solution)/shard_map/ppermute | solution.py:231
  11.2 1.8 %collective-permute-done.came = f32[1088,128]{1,0:T(8,128)S(1)} collective-permute-done((f32[1088,128]{1,0:T(8,128)}, f32[1088,128]{1,0:T(8,128)S(1)}, u32[]{:S(2)}, u32[]{:S(2)}) %collective-permute-start) | collective-permute-done | bytes 557088 | tf_op jit(solution)/shard_map/ppermute | solution.py:231
  13.0 0.0 copy-start.1
  13.0 0.8 copy-done.1
  13.8 2.2 %pack.1 = f32[8,192,128]{2,1,0:T(8,128)} custom-call(f32[1088,128]{1,0:T(8,128)} %get-tuple-element.18.keep, f32[1088,128]{1,0:T(8,128)} %copy-done.1), custom_call_target="tpu_custom_call" | custom-call | tf_op jit(solution)/shard_map/pack/pallas_call | solution.py:232
  16.0 20.5 %all_to_all.20.came = f32[8,192,128]{2,1,0:T(8,128)} all-to-all(f32[8,192,128]{2,1,0:T(8,128)} %pack.1), channel_id=1, replica_groups=mesh['y'=4,'xl'=2,'xh'=2,'z'=4,'c'=2] {'xh','z'}, dimensions={0} | all-to-all | bytes 1572864 | tf_op jit(solution)/shard_map/all_to_all | solution.py:235
  36.5 2.1 %group.1 = (f32[8,128,128]{2,1,0:T(8,128)}, f32[2,64,128]{2,1,0:T(8,128)}, f32[2,64,64]{2,1,0:T(8,128)}) custom-call(f32[8,192,128]{2,1,0:T(8,128)} %all_to_all.20.came, f32[64,128]{1,0:T(8,128)} %get-tuple-element.20.v_own), custom_call_target="tpu_custom_call" | custom-call | tf_op jit(solution)/shard_map/group/pallas_call | solution.py:236
  38.6 11.7 %all_to_all.21.came = f32[8,128,128]{2,1,0:T(8,128)} all-to-all(f32[8,128,128]{2,1,0:T(8,128)} %get-tuple-element.21), channel_id=1, replica_groups=mesh['y'=4,'xl'=2,'xh'=2,'z'=4,'c'=2] {'y','xl'}, dimensions={0} | all-to-all | bytes 1048576 | tf_op jit(solution)/shard_map/all_to_all | solution.py:243
  50.3 3.2 %first.1 = (f32[8,64,128]{2,1,0:T(8,128)}, f32[64,128]{1,0:T(8,128)}, f32[64,128]{1,0:T(8,128)}, f32[64,64]{1,0:T(8,128)}) custom-call(f32[8,128,128]{2,1,0:T(8,128)} %all_to_all.21.came, f32[2,64,128]{2,1,0:T(8,128)} %get-tuple-element.22.stats, f32[2,64,64]{2,1,0:T(8,128)} %get-tuple-element.23.grams, f32[64,128]{1,0:T(8,128)} %get-tuple-element.24.w_own, ...), custom_call_target="tpu_custom_call" | custom-call | tf_op jit(solution)/shard_map/first/pallas_call | solution.py:244
  53.5 10.2 %all_to_all.22.came = f32[8,64,128]{2,1,0:T(8,128)} all-to-all(f32[8,64,128]{2,1,0:T(8,128)} %get-tuple-element.25), channel_id=1, replica_groups=mesh['y'=4,'xl'=2,'xh'=2,'z'=4,'c'=2] {'y','xl'}, dimensions={0} | all-to-all | bytes 524288 | tf_op jit(solution)/shard_map/all_to_all | solution.py:251
  63.7 2.9 %second.1 = f32[8,128,128]{2,1,0:T(8,128)} custom-call(f32[8,64,128]{2,1,0:T(8,128)} %all_to_all.22.came, f32[2,64,128]{2,1,0:T(8,128)} %get-tuple-element.22.stats, f32[2,64,64]{2,1,0:T(8,128)} %get-tuple-element.23.grams, f32[64,128]{1,0:T(8,128)} %get-tuple-element.26.w_own, f32[64,128]{1,0:T(8,128)} %get-tuple-element.27.v_own, ...), custom_call_target="tpu_custom_call" | custom-call | tf_op jit(solution)/shard_map/second/pallas_call | solution.py:252
  66.6 14.4 %all_to_all.23.mine = f32[8,128,128]{2,1,0:T(8,128)S(1)} all-to-all(f32[8,128,128]{2,1,0:T(8,128)} %second.1), channel_id=1, replica_groups=mesh['y'=4,'xl'=2,'xh'=2,'z'=4,'c'=2] {'xh','z'}, dimensions={0} | all-to-all | bytes 1048576 | tf_op jit(solution)/shard_map/all_to_all | solution.py:255
  80.9 0.0 copy-start
  80.9 4.6 %collective-permute-start.1 = (f32[8,128,128]{2,1,0:T(8,128)S(1)}, f32[8,128,128]{2,1,0:T(8,128)S(1)}, u32[]{:S(2)}, u32[]{:S(2)}) collective-permute-start(f32[8,128,128]{2,1,0:T(8,128)S(1)} %all_to_all.23.mine), channel_id=1, source_target_pairs={{0,1},{1,0},{2,3},{3,2},{4,5},{5,4},{6,7},{7,6},{8,9},{9,8},{10,11... | collective-permute-start | bytes 1572872 | tf_op jit(solution)/shard_map/ppermute | solution.py:256
  85.5 1.5 %collective-permute-done.1.other = f32[8,128,128]{2,1,0:T(8,128)S(1)} collective-permute-done((f32[8,128,128]{2,1,0:T(8,128)S(1)}, f32[8,128,128]{2,1,0:T(8,128)S(1)}, u32[]{:S(2)}, u32[]{:S(2)}) %collective-permute-start.1) | collective-permute-done | bytes 524320 | tf_op jit(solution)/shard_map/ppermute | solution.py:256
  87.0 0.0 copy-done
  87.0 0.0 copy-start.2
  87.0 0.8 copy-done.2
  87.8 2.3 %finish.1 = (f32[64,2000]{1,0:T(8,128)}, f32[1,64,2000]{2,1,0:T(8,128)}) custom-call(s32[2]{0:T(128)} %pad_add_fusion.where, f32[8,128,128]{2,1,0:T(8,128)} %copy-done, f32[8,128,128]{2,1,0:T(8,128)} %copy-done.2), custom_call_target="tpu_custom_call" | custom-call | tf_op jit(solution)/shard_map/finish/pallas_call | solution.py:257
Async XLA Ops:
  9.8 3.2 %collective-permute-start = (f32[1088,128]{1,0:T(8,128)}, f32[1088,128]{1,0:T(8,128)S(1)}, u32[]{:S(2)}, u32[]{:S(2)}) collective-permute-start(f32[1088,128]{1,0:T(8,128)} %get-tuple-element.19), channel_id=1, source_target_pairs={{0,1},{1,0},{2,3},{3,2},{4,5},{5,4},{6,7},{7,6},{8,9},{9,8},{10,11... | collective-permute-start | bytes 1671176 | tf_op jit(solution)/shard_map/ppermute | solution.py:231
  13.0 0.8 copy-start.1
  80.9 6.1 %copy-start = (f32[8,128,128]{2,1,0:T(8,128)}, f32[8,128,128]{2,1,0:T(8,128)S(1)}, u32[]{:S(2)}) copy-start(f32[8,128,128]{2,1,0:T(8,128)S(1)} %all_to_all.23.mine) | copy-start | bytes 1572868
  80.9 6.1 %collective-permute-start.1 = (f32[8,128,128]{2,1,0:T(8,128)S(1)}, f32[8,128,128]{2,1,0:T(8,128)S(1)}, u32[]{:S(2)}, u32[]{:S(2)}) collective-permute-start(f32[8,128,128]{2,1,0:T(8,128)S(1)} %all_to_all.23.mine), channel_id=1, source_target_pairs={{0,1},{1,0},{2,3},{3,2},{4,5},{5,4},{6,7},{7,6},{8,9},{9,8},{10,11... | collective-permute-start | bytes 1572872 | tf_op jit(solution)/shard_map/ppermute | solution.py:256
  87.0 0.8 copy-start.2

commit v2 on v1

--- a/solution.py
+++ b/solution.py
@@ -52,8 +52,9 @@
     return state
 
 
-def front_kernel(where, dmap, sweeps, x, picks, w, v, loads, keep, send, w_own, v_own, table):
-    core, tile = where[0], where[1]
+def front_kernel(dmap, sweeps, x, picks, w, v, loads, keep, send, w_own, v_own, table):
+    core = lax.axis_index("c")
+    tile = core * 8 + lax.axis_index("xh") * 4 + lax.axis_index("z")
     count = sweeps[dmap[0]]
     shared, specific = w[...], v[0]
     mixed = shared + specific
@@ -129,67 +130,107 @@
         out[i, N:] = gram
 
 
-def group_kernel(came, v_own, out, stats, grams):
+def group_kernel(came, v_own, out):
     total = came[0]
     for i in range(1, 8):
         total = total + came[i]
     rows = total[:N].T
-    first = rows[:K]
-    stats[0] = first
-    stats[1] = first + rows[K:]
+    first, second = rows[:K], rows[:K] + rows[K:]
     gram = total[N:]
-    grams[0] = gram[:, :K]
-    grams[1] = gram[:, :K] + gram[:, K:]
-    carried = first - jnp.dot(gram[:, :K], v_own[...], precision=HIGHEST, preferred_element_type=F32)
+    lanes = lax.broadcasted_iota(jnp.int32, (K, N), 1)
+    early = pltpu.roll(gram, K, 1)
+    grams = jnp.where(lanes < K, gram, gram + early)
+    specific = v_own[...]
     for i in range(8):
-        out[i, :K] = carried
-        out[i, K:] = gram
-
-
-def renew(w, v, gram_total, gram, carried, stat):
-    inverse = 1.0 / jnp.maximum(diagonal(gram_total), 1.0)
-    scaled = gram_total * inverse
-    start = carried - jnp.dot(gram_total, w, precision=HIGHEST, preferred_element_type=F32)
-    state, residual = [rows_of(w)], [rows_of(start * inverse)]
-
-    def columns(table):
-        return lambda k: rows_of(jnp.broadcast_to(table[:, k : k + 1], (K, N)))
-
-    coordinate_steps(state, residual, columns(scaled))
-    w_next = jnp.concatenate(state[0], axis=0)
-    own_inverse = 1.0 / jnp.maximum(RIDGE * diagonal(gram), 1.0)
-    own_scaled = (RIDGE * gram) * own_inverse
-    pulled = jnp.dot(gram, w_next + RIDGE * v, precision=HIGHEST, preferred_element_type=F32)
-    state, residual = [rows_of(v)], [rows_of((stat - pulled) * own_inverse)]
-    coordinate_steps(state, residual, columns(own_scaled))
-    return w_next, jnp.concatenate(state[0], axis=0)
-
-
-def first_kernel(came, stats, grams, w_own, v_own, out, w_next, v_next, gram_total):
-    total = came[0]
+        out[i, :K] = first
+        out[i, K:N] = second
+        out[i, N : N + K] = grams
+        out[i, N + K :] = specific
+
+
+def dot_split(a, b):
+    a_high = a.astype(BF16)
+    b_high = b.astype(BF16)
+    a_low = (a - a_high.astype(F32)).astype(BF16)
+    b_low = (b - b_high.astype(F32)).astype(BF16)
+    out = jnp.dot(a_high, b_low, preferred_element_type=F32)
+    out = out + jnp.dot(a_low, b_high, preferred_element_type=F32)
+    return out + jnp.dot(a_high, b_high, preferred_element_type=F32)
+
+
+def one_pass(state, residual, tables, first_lane):
+    sub = lax.broadcasted_iota(jnp.int32, (8, N), 0)
+    for k in range(K):
+        t, s = divmod(k, 8)
+        lane = first_lane + k
+        for h, r, table in zip(state, residual, tables):
+            change = jnp.maximum(-h[t], r[t])
+            spread = jnp.broadcast_to(change[s : s + 1], (8, N))
+            h[t] = jnp.where(sub == s, h[t] + change, h[t])
+            for j in range(t if s < 7 else t + 1, K // 8):
+                weight = jnp.broadcast_to(table[8 * j : 8 * j + 8, lane : lane + 1], (8, N))
+                r[j] = r[j] - weight * spread
+    return [jnp.concatenate(h, axis=0) for h in state]
+
+
+def update_kernel(came, w_own, out, v_first):
+    group = lax.axis_index("y") * 2 + lax.axis_index("xl")
+    zero = jnp.zeros((K, N), F32)
+    stat = came[0, :K]
+    stat_next = came[0, K:N]
+    total = came[0, N : N + K]
     for i in range(1, 8):
-        total = total + came[i]
-    all_grams = total[K:]
-    gram_total[...] = all_grams[:, :K] + all_grams[:, K:]
-    shared, specific = renew(w_own[...], v_own[...], all_grams[:, :K], grams[0], total[:K], stats[0])
-    w_next[...] = shared
-    v_next[...] = specific
-    carried = stats[1] - jnp.dot(grams[1], specific, precision=HIGHEST, preferred_element_type=F32)
+        stat = stat + came[i, :K]
+        stat_next = stat_next + came[i, K:N]
+        total = total + came[i, N : N + K]
+    grams = [came[i, N : N + K] for i in range(8)]
+
+    def scaled_of(gram, scale, at):
+        inverse = 1.0 / jnp.maximum(scale * diagonal(gram[:, at : at + K]), 1.0)
+        return (scale * gram) * inverse, inverse
+
+    pulls = [dot_split(grams[i], jnp.concatenate([came[i, N + K :], zero], axis=0)) for i in range(8)]
+    carried = stat
     for i in range(8):
-        out[i] = carried
-
-
-def second_kernel(came, stats, grams, w_own, v_own, gram_total, out):
-    total = came[0]
-    for i in range(1, 8):
-        total = total + came[i]
-    shared, specific = renew(w_own[...], v_own[...], gram_total[...], grams[1], total, stats[1])
+        carried = carried - pulls[i]
+    shared = w_own[...]
+    table, inverse = scaled_of(total, 1.0, 0)
+    start = carried - dot_split(total, jnp.concatenate([shared, zero], axis=0))
+    (shared,) = one_pass([rows_of(shared)], [rows_of(start * inverse)], [table], 0)
+
+    stacked = jnp.concatenate(grams, axis=0)
+    pushed = dot_split(stacked, jnp.concatenate([shared, zero], axis=0))
+    for pair in range(0, 8, 4):
+        state, residual, tables = [], [], []
+        for i in range(pair, pair + 4):
+            table, inverse = scaled_of(grams[i], RIDGE, 0)
+            rest = came[i, :K] - pushed[K * i : K * i + K] - RIDGE * pulls[i]
+            state.append(rows_of(came[i, N + K :]))
+            residual.append(rows_of(rest * inverse))
+            tables.append(table)
+        for i, value in enumerate(one_pass(state, residual, tables, 0)):
+            v_first[pair + i] = value
+
+    wide = jnp.concatenate(grams, axis=1)
+    tall = jnp.concatenate([part for i in range(8) for part in (zero, v_first[i])], axis=0)
+    carried = stat_next - dot_split(wide, tall)
+    table, inverse = scaled_of(total, 1.0, K)
+    start = carried - dot_split(total, jnp.concatenate([zero, shared], axis=0))
+    (shared,) = one_pass([rows_of(shared)], [rows_of(start * inverse)], [table], K)
+
+    gram = came[group, N : N + K]
+    specific = v_first[group]
+    table, inverse = scaled_of(gram, RIDGE, K)
+    rest = came[group, K:N] - dot_split(gram, jnp.concatenate([zero, shared + RIDGE * specific], axis=0))
+    (specific,) = one_pass([rows_of(specific)], [rows_of(rest * inverse)], [table], K)
     for i in range(8):
         out[i, :K] = shared
         out[i, K:] = specific
 
 
-def finish_kernel(where, mine, other, w, v):
+def finish_kernel(mine, other, w, v):
+    core = lax.axis_index("c")
+
     def write(first, second):
         for half, part in enumerate((first, second)):
             for i in range(8):
@@ -198,17 +239,25 @@
                 w[:, at : at + wide] = part[i, :K, :wide]
                 v[0, :, at : at + wide] = part[i, K:, :wide]
 
-    @pl.when(where[0] == 0)
+    @pl.when(core == 0)
     def _():
         write(mine, other)
 
-    @pl.when(where[0] == 1)
+    @pl.when(core == 1)
     def _():
         write(other, mine)
 
 
 def shape(*dims):
     return jax.ShapeDtypeStruct(dims, F32)
+
+
+def near(*dims):
+    return pltpu.VMEM(dims, F32)
+
+
+def held(x):
+    return pltpu.with_memory_space_constraint(x, pltpu.VMEM)
 
 
 VM = pl.BlockSpec(memory_space=pltpu.VMEM)
@@ -217,50 +266,40 @@
 
 
 def on_device(expression, dataset_id, dataset_map, sweep_count, picks, shared_init, specific_init):
-    core = lax.axis_index("c")
-    tile = core * 8 + lax.axis_index("xh") * 4 + lax.axis_index("z")
-    where = jnp.stack([core, tile]).astype(jnp.int32)
     loads, keep, send, w_own, v_own = pl.pallas_call(
         front_kernel,
         name="front",
-        out_shape=(shape(2, K, N), shape(HALF + K, N), shape(HALF + K, N), shape(K, N), shape(K, N)),
-        in_specs=[SM, SM, SM, VM, VM, VM, VM],
+        out_shape=(shape(2, K, N), near(HALF + K, N), near(HALF + K, N), near(K, N), near(K, N)),
+        in_specs=[SM, SM, VM, VM, VM, VM],
         out_specs=[VM] * 5,
         scratch_shapes=[pltpu.VMEM((K, K, N), F32)],
-    )(where, dataset_map, sweep_count, expression, picks, shared_init, specific_init)
+    )(dataset_map, sweep_count, expression, picks, shared_init, specific_init)
     came = lax.ppermute(send, "c", SWAP)
     packed = pl.pallas_call(
-        pack_kernel, name="pack", out_shape=shape(8, N + K, N), in_specs=[VM, VM], out_specs=VM
-    )(keep, came)
+        pack_kernel, name="pack", out_shape=near(8, N + K, N), in_specs=[VM, VM], out_specs=VM
+    )(held(keep), held(came))
     came = lax.all_to_all(packed, RING, 0, 0, tiled=True)
-    spread, stats, grams = pl.pallas_call(
-        group_kernel,
-        name="group",
-        out_shape=(shape(8, N, N), shape(2, K, N), shape(2, K, K)),
-        in_specs=[VM, VM],
-        out_specs=[VM] * 3,
-    )(came, v_own)
-    came = lax.all_to_all(spread, GRP, 0, 0, tiled=True)
-    spread, w_own, v_own, gram_total = pl.pallas_call(
-        first_kernel,
-        name="first",
-        out_shape=(shape(8, K, N), shape(K, N), shape(K, N), shape(K, K)),
-        in_specs=[VM] * 5,
-        out_specs=[VM] * 4,
-    )(came, stats, grams, w_own, v_own)
+    spread = pl.pallas_call(
+        group_kernel, name="group", out_shape=near(8, 2 * N, N), in_specs=[VM, VM], out_specs=VM
+    )(held(came), held(v_own))
     came = lax.all_to_all(spread, GRP, 0, 0, tiled=True)
     spread = pl.pallas_call(
-        second_kernel, name="second", out_shape=shape(8, N, N), in_specs=[VM] * 6, out_specs=VM
-    )(came, stats, grams, w_own, v_own, gram_total)
+        update_kernel,
+        name="update",
+        out_shape=near(8, N, N),
+        in_specs=[VM, VM],
+        out_specs=VM,
+        scratch_shapes=[pltpu.VMEM((8, K, N), F32)],
+    )(held(came), held(w_own))
     mine = lax.all_to_all(spread, RING, 0, 0, tiled=True)
     other = lax.ppermute(mine, "c", SWAP)
     shared, specific = pl.pallas_call(
         finish_kernel,
         name="finish",
         out_shape=(shape(K, G), shape(1, K, G)),
-        in_specs=[SM, VM, VM],
+        in_specs=[VM, VM],
         out_specs=[VM, VM],
-    )(where, mine, other)
+    )(held(mine), held(other))
     return loads, shared, specific
 
 

time: 91.1 us -> 76.6 us (0.84)
  Pallas kernels: 20.6 us -> 14.6 us
  blocking collectives: 56.7 us -> 52.5 us
  local copies, waits for them, and re-layouts: 1.62 us -> 0 us
  starting transfers between devices: 5.94 us -> 4.92 us
    pallas_call x5 -> x4, Pallas kernels: 18.3 us -> 13.5 us  [the longest x1 7.08 us: on_device(): pl.pallas_call(front_kernel, name='front', out_shape=(shape(2, K, N), nea...]
    all_to_all x2 -> x1, blocking collectives: 21.8 us -> 17.5 us  [on_device(): came = lax.all_to_all(spread, GRP, 0, 0, tiled=True)]
    unnamed x6 -> x0, local copies, waits for them, and re-layouts: 1.62 us -> none
    pallas_call x1, Pallas kernels: 2.29 us -> 1.07 us  [on_device(): pl.pallas_call(finish_kernel, name='finish', out_shape=(shape(K, G), shap...]
    ppermute x1, starting transfers between devices: 4.57 us -> 3.56 us  [on_device(): other = lax.ppermute(mine, 'c', SWAP)]
where the time goes in v2:
time: 76.6 us; the launch traced here: 76.4 us
  blocking collectives  52.5 us (69%)
  Pallas kernels  14.6 us (19%)
  starting transfers between devices  4.92 us (6%)
  waiting for transfers between devices  3.12 us (4%)
  between operations  1.3 us (2%)
    all_to_all x1, blocking collectives, on_device(): came = lax.all_to_all(packed, RING, 0, 0, tiled=True)  20.2 us
    all_to_all x1, blocking collectives, on_device(): came = lax.all_to_all(spread, GRP, 0, 0, tiled=True)  17.5 us
    all_to_all x1, blocking collectives, on_device(): mine = lax.all_to_all(spread, RING, 0, 0, tiled=True)  14.8 us
    pallas_call x1, Pallas kernels, on_device(): pl.pallas_call(front_kernel, name='front', out_shape=(shape(2, K, N), nea...  7.08 us
    pallas_call x1, Pallas kernels, on_device(): pl.pallas_call(update_kernel, name='update', out_shape=near(8, N, N), in_...  6.2 us
    ppermute x1, starting transfers between devices, on_device(): other = lax.ppermute(mine, 'c', SWAP)  3.56 us
    ppermute x1, waiting for transfers between devices, on_device(): came = lax.ppermute(send, 'c', SWAP)  1.58 us
    ppermute x1, waiting for transfers between devices, on_device(): other = lax.ppermute(mine, 'c', SWAP)  1.54 us
  transfers between devices with their start and end apart: 2, of which 2 were waited for; matrix products, arithmetic and copies ran while one was open for 0% of the time, Pallas kernels for 0%

profile of v2, /device:TPU:1, one launch (start us, length us, event | category | flops | bytes accessed | tf_op | source)
XLA Modules:
  0.0 76.4 jit_solution(12936807531806503445)
XLA Ops:
  1.3 7.1 %front.1 = (f32[2,64,128]{2,1,0:T(8,128)}, f32[1088,128]{1,0:T(8,128)S(1)}, f32[1088,128]{1,0:T(8,128)S(1)}, f32[64,128]{1,0:T(8,128)S(1)}, f32[64,128]{1,0:T(8,128)S(1)}) custom-call(s32[1]{0:T(128)S(6)} %copy.9.dmap, s32[8]{0:T(128)} %sweeps.1, bf16[2000,512]{1,0:T(8,128)(2,1)} %x.1, s32[2,128]{1,0:T(2,128)} %picks.1, f32[64,2000]{1,0:T(8,128)} %w.1, ...), custom_call_target="tpu_custom_call" | custom-call | tf_op jit(solution)/shard_map/front/pallas_call | solution.py:269
  8.4 1.4 %collective-permute-start = (f32[1088,128]{1,0:T(8,128)S(1)}, f32[1088,128]{1,0:T(8,128)S(1)}, u32[]{:S(2)}, u32[]{:S(2)}) collective-permute-start(f32[1088,128]{1,0:T(8,128)S(1)} %get-tuple-element.12), channel_id=1, source_target_pairs={{0,1},{1,0},{2,3},{3,2},{4,5},{5,4},{6,7},{7,6},{8,9},{9,8},{10,11... | collective-permute-start | bytes 1671176 | tf_op jit(solution)/shard_map/ppermute | solution.py:277
  9.7 1.6 %collective-permute-done.came = f32[1088,128]{1,0:T(8,128)S(1)} collective-permute-done((f32[1088,128]{1,0:T(8,128)S(1)}, f32[1088,128]{1,0:T(8,128)S(1)}, u32[]{:S(2)}, u32[]{:S(2)}) %collective-permute-start) | collective-permute-done | bytes 557088 | tf_op jit(solution)/shard_map/ppermute | solution.py:277
  11.3 0.1 pack.1
  11.4 20.2 %all_to_all.15.came = f32[8,192,128]{2,1,0:T(8,128)S(1)} all-to-all(f32[8,192,128]{2,1,0:T(8,128)S(1)} %pack.1), channel_id=1, replica_groups=mesh['y'=4,'xl'=2,'xh'=2,'z'=4,'c'=2] {'xh','z'}, dimensions={0} | all-to-all | bytes 1572864 | tf_op jit(solution)/shard_map/all_to_all | solution.py:281
  31.6 0.1 group.1
  31.8 17.5 %all_to_all.16.came = f32[8,256,128]{2,1,0:T(8,128)S(1)} all-to-all(f32[8,256,128]{2,1,0:T(8,128)S(1)} %group.1), channel_id=1, replica_groups=mesh['y'=4,'xl'=2,'xh'=2,'z'=4,'c'=2] {'y','xl'}, dimensions={0} | all-to-all | bytes 2097152 | tf_op jit(solution)/shard_map/all_to_all | solution.py:285
  49.3 6.2 %update.1 = f32[8,128,128]{2,1,0:T(8,128)S(1)} custom-call(f32[8,256,128]{2,1,0:T(8,128)S(1)} %all_to_all.16.came, f32[64,128]{1,0:T(8,128)S(1)} %get-tuple-element.14.w_own), custom_call_target="tpu_custom_call" | custom-call | tf_op jit(solution)/shard_map/update/pallas_call | solution.py:286
  55.5 14.8 %all_to_all.17.mine = f32[8,128,128]{2,1,0:T(8,128)S(1)} all-to-all(f32[8,128,128]{2,1,0:T(8,128)S(1)} %update.1), channel_id=1, replica_groups=mesh['y'=4,'xl'=2,'xh'=2,'z'=4,'c'=2] {'xh','z'}, dimensions={0} | all-to-all | bytes 1048576 | tf_op jit(solution)/shard_map/all_to_all | solution.py:294
  70.2 3.6 %collective-permute-start.1 = (f32[8,128,128]{2,1,0:T(8,128)S(1)}, f32[8,128,128]{2,1,0:T(8,128)S(1)}, u32[]{:S(2)}, u32[]{:S(2)}) collective-permute-start(f32[8,128,128]{2,1,0:T(8,128)S(1)} %all_to_all.17.mine), channel_id=1, source_target_pairs={{0,1},{1,0},{2,3},{3,2},{4,5},{5,4},{6,7},{7,6},{8,9},{9,8},{10,11... | collective-permute-start | bytes 1572872 | tf_op jit(solution)/shard_map/ppermute | solution.py:295
  73.8 1.5 %collective-permute-done.1.other = f32[8,128,128]{2,1,0:T(8,128)S(1)} collective-permute-done((f32[8,128,128]{2,1,0:T(8,128)S(1)}, f32[8,128,128]{2,1,0:T(8,128)S(1)}, u32[]{:S(2)}, u32[]{:S(2)}) %collective-permute-start.1) | collective-permute-done | bytes 524320 | tf_op jit(solution)/shard_map/ppermute | solution.py:295
  75.3 1.1 %finish.1 = (f32[64,2000]{1,0:T(8,128)}, f32[1,64,2000]{2,1,0:T(8,128)}) custom-call(f32[8,128,128]{2,1,0:T(8,128)S(1)} %all_to_all.17.mine, f32[8,128,128]{2,1,0:T(8,128)S(1)} %collective-permute-done.1.other), custom_call_target="tpu_custom_call" | custom-call | tf_op jit(solution)/shard_map/finish/pallas_call | solution.py:296
Async XLA Ops:
  8.4 2.9 %collective-permute-start = (f32[1088,128]{1,0:T(8,128)S(1)}, f32[1088,128]{1,0:T(8,128)S(1)}, u32[]{:S(2)}, u32[]{:S(2)}) collective-permute-start(f32[1088,128]{1,0:T(8,128)S(1)} %get-tuple-element.12), channel_id=1, source_target_pairs={{0,1},{1,0},{2,3},{3,2},{4,5},{5,4},{6,7},{7,6},{8,9},{9,8},{10,11... | collective-permute-start | bytes 1671176 | tf_op jit(solution)/shard_map/ppermute | solution.py:277
  70.2 5.1 %collective-permute-start.1 = (f32[8,128,128]{2,1,0:T(8,128)S(1)}, f32[8,128,128]{2,1,0:T(8,128)S(1)}, u32[]{:S(2)}, u32[]{:S(2)}) collective-permute-start(f32[8,128,128]{2,1,0:T(8,128)S(1)} %all_to_all.17.mine), channel_id=1, source_target_pairs={{0,1},{1,0},{2,3},{3,2},{4,5},{5,4},{6,7},{7,6},{8,9},{9,8},{10,11... | collective-permute-start | bytes 1572872 | tf_op jit(solution)/shard_map/ppermute | solution.py:295

commit v3 on v2

--- a/solution.py
+++ b/solution.py
@@ -9,6 +9,7 @@
 G = 2000
 N = 128
 HALF = 8 * N
+PACKED = K // 2 + 8
 LAST = G - 15 * N
 EPSILON = 1e-06
 LAMBDA = 5.0
@@ -16,6 +17,7 @@
 HIGHEST = lax.Precision.HIGHEST
 GRP = ("y", "xl")
 RING = ("xh", "z")
+PLANE = ("xl", "xh", "z")
 ALL = ("y", "xl", "xh", "z", "c")
 NT = (((1,), (1,)), ((), ()))
 F32 = jnp.float32
@@ -52,6 +54,56 @@
     return state
 
 
+def lanes_of(rows):
+    return lax.broadcasted_iota(jnp.int32, (rows, N), 1)
+
+
+def swapped(x):
+    return pltpu.roll(x, K, 1)
+
+
+def left_left(a, b):
+    return jnp.where(lanes_of(a.shape[0]) < K, a, swapped(b))
+
+
+def right_right(a, b):
+    return jnp.where(lanes_of(a.shape[0]) < K, swapped(a), b)
+
+
+def split_rows(x):
+    return left_left(x[: K // 2], x[K // 2 :]), right_right(x[: K // 2], x[K // 2 :])
+
+
+def pair_rows(a, b):
+    return jnp.concatenate([left_left(a, b), right_right(a, b)], axis=0)
+
+
+def corners(x):
+    left = lanes_of(K) < K
+    return jnp.concatenate([jnp.where(left, x, 0.0), jnp.where(left, 0.0, x)], axis=0)
+
+
+def fold_grams(gram):
+    rows = lax.broadcasted_iota(jnp.int32, (K, N), 0)
+    other = swapped(gram)
+    square = jnp.where(lanes_of(K) <= rows, gram, other)
+    packed = left_left(square[: K // 2], square[K // 2 :])
+    diag = jnp.sum(jnp.where(lanes_of(K) == rows, other, 0.0), axis=0, keepdims=True)
+    return jnp.concatenate([packed, jnp.broadcast_to(diag, (8, N))], axis=0)
+
+
+def unfold_grams(a, b):
+    square = pair_rows(a[: K // 2], b[: K // 2])
+    turned = corners(square).T
+    turned = turned[:K] + turned[K:]
+    diag = left_left(a[K // 2 :], b[K // 2 :])[:1]
+    rows = lax.broadcasted_iota(jnp.int32, (K, N), 0)
+    cols = lanes_of(K) % K
+    first = jnp.where(cols <= rows, square, turned)
+    second = jnp.where(cols < rows, turned, jnp.where(cols == rows, diag, square))
+    return first, first + second
+
+
 def front_kernel(dmap, sweeps, x, picks, w, v, loads, keep, send, w_own, v_own, table):
     core = lax.axis_index("c")
     tile = core * 8 + lax.axis_index("xh") * 4 + lax.axis_index("z")
@@ -103,7 +155,7 @@
     block = jnp.concatenate(
         [jnp.concatenate([first, zero], axis=1), jnp.concatenate([zero, second], axis=1)], axis=0
     )
-    gram_part = dot_nt(both, block, HIGHEST)
+    gram_part = fold_grams(dot_nt(both, block, HIGHEST))
     keep[HALF:] = gram_part
     send[HALF:] = gram_part
     rounded = block.astype(BF16)
@@ -136,16 +188,12 @@
         total = total + came[i]
     rows = total[:N].T
     first, second = rows[:K], rows[:K] + rows[K:]
-    gram = total[N:]
-    lanes = lax.broadcasted_iota(jnp.int32, (K, N), 1)
-    early = pltpu.roll(gram, K, 1)
-    grams = jnp.where(lanes < K, gram, gram + early)
-    specific = v_own[...]
+    stats = (left_left(first, second), right_right(first, second))
+    bases = split_rows(v_own[...])
     for i in range(8):
-        out[i, :K] = first
-        out[i, K:N] = second
-        out[i, N : N + K] = grams
-        out[i, N + K :] = specific
+        out[i, :K] = stats[i % 2]
+        out[i, K : K + K // 2] = bases[i % 2]
+        out[i, K + K // 2 :] = total[N:]
 
 
 def dot_split(a, b):
@@ -158,74 +206,85 @@
     return out + jnp.dot(a_high, b_high, preferred_element_type=F32)
 
 
-def one_pass(state, residual, tables, first_lane):
+def one_pass(state, residual, tables, paired):
     sub = lax.broadcasted_iota(jnp.int32, (8, N), 0)
+    half = jnp.where(lanes_of(8) < K, 0, K)
     for k in range(K):
         t, s = divmod(k, 8)
-        lane = first_lane + k
         for h, r, table in zip(state, residual, tables):
             change = jnp.maximum(-h[t], r[t])
             spread = jnp.broadcast_to(change[s : s + 1], (8, N))
             h[t] = jnp.where(sub == s, h[t] + change, h[t])
             for j in range(t if s < 7 else t + 1, K // 8):
-                weight = jnp.broadcast_to(table[8 * j : 8 * j + 8, lane : lane + 1], (8, N))
+                weight = table[8 * j : 8 * j + 8]
+                if paired:
+                    weight = jnp.take_along_axis(weight, half + k, axis=1, mode="promise_in_bounds")
+                else:
+                    weight = jnp.broadcast_to(weight[:, k : k + 1], (8, N))
                 r[j] = r[j] - weight * spread
     return [jnp.concatenate(h, axis=0) for h in state]
 
 
-def update_kernel(came, w_own, out, v_first):
-    group = lax.axis_index("y") * 2 + lax.axis_index("xl")
-    zero = jnp.zeros((K, N), F32)
-    stat = came[0, :K]
-    stat_next = came[0, K:N]
-    total = came[0, N : N + K]
-    for i in range(1, 8):
-        stat = stat + came[i, :K]
-        stat_next = stat_next + came[i, K:N]
-        total = total + came[i, N : N + K]
-    grams = [came[i, N : N + K] for i in range(8)]
-
-    def scaled_of(gram, scale, at):
-        inverse = 1.0 / jnp.maximum(scale * diagonal(gram[:, at : at + K]), 1.0)
-        return (scale * gram) * inverse, inverse
-
-    pulls = [dot_split(grams[i], jnp.concatenate([came[i, N + K :], zero], axis=0)) for i in range(8)]
-    carried = stat
-    for i in range(8):
-        carried = carried - pulls[i]
-    shared = w_own[...]
-    table, inverse = scaled_of(total, 1.0, 0)
-    start = carried - dot_split(total, jnp.concatenate([shared, zero], axis=0))
-    (shared,) = one_pass([rows_of(shared)], [rows_of(start * inverse)], [table], 0)
-
-    stacked = jnp.concatenate(grams, axis=0)
-    pushed = dot_split(stacked, jnp.concatenate([shared, zero], axis=0))
-    for pair in range(0, 8, 4):
-        state, residual, tables = [], [], []
-        for i in range(pair, pair + 4):
-            table, inverse = scaled_of(grams[i], RIDGE, 0)
-            rest = came[i, :K] - pushed[K * i : K * i + K] - RIDGE * pulls[i]
-            state.append(rows_of(came[i, N + K :]))
-            residual.append(rows_of(rest * inverse))
-            tables.append(table)
-        for i, value in enumerate(one_pass(state, residual, tables, 0)):
-            v_first[pair + i] = value
-
-    wide = jnp.concatenate(grams, axis=1)
-    tall = jnp.concatenate([part for i in range(8) for part in (zero, v_first[i])], axis=0)
-    carried = stat_next - dot_split(wide, tall)
-    table, inverse = scaled_of(total, 1.0, K)
-    start = carried - dot_split(total, jnp.concatenate([zero, shared], axis=0))
-    (shared,) = one_pass([rows_of(shared)], [rows_of(start * inverse)], [table], K)
-
-    gram = came[group, N : N + K]
-    specific = v_first[group]
-    table, inverse = scaled_of(gram, RIDGE, K)
-    rest = came[group, K:N] - dot_split(gram, jnp.concatenate([zero, shared + RIDGE * specific], axis=0))
-    (specific,) = one_pass([rows_of(specific)], [rows_of(rest * inverse)], [table], K)
-    for i in range(8):
-        out[i, :K] = shared
-        out[i, K:] = specific
+def both_halves(x):
+    return x + swapped(x)
+
+
+def shared_pass(shared, gram, carried):
+    inverse = 1.0 / jnp.maximum(diagonal(gram[:, :K]), 1.0)
+    start = carried - dot_split(gram, jnp.concatenate([shared, jnp.zeros((K, N), F32)], axis=0))
+    return one_pass([rows_of(shared)], [rows_of(start * inverse)], [gram * inverse], False)[0]
+
+
+def ridge_scale(gram):
+    rows = lax.broadcasted_iota(jnp.int32, (K, N), 0)
+    left = jnp.sum(jnp.where(lanes_of(K) == rows, gram, 0.0), axis=1, keepdims=True)
+    right = jnp.sum(jnp.where(lanes_of(K) == rows + K, gram, 0.0), axis=1, keepdims=True)
+    return 1.0 / jnp.maximum(RIDGE * jnp.where(lanes_of(K) < K, left, right), 1.0)
+
+
+def update_kernel(came, w_own, out, stats, grams_next, v_first):
+    at_y, at_xl = lax.axis_index("y"), lax.axis_index("xl")
+    pairs = range(4)
+    stat, base, grams = [], [], []
+    for p in pairs:
+        a, b = 2 * p, 2 * p + 1
+        stat.append(left_left(came[a, :K], came[b, :K]))
+        stats[p] = right_right(came[a, :K], came[b, :K])
+        base.append(pair_rows(came[a, K : K + K // 2], came[b, K : K + K // 2]))
+        first, both = unfold_grams(came[a, K + K // 2 :], came[b, K + K // 2 :])
+        grams.append(first)
+        grams_next[p] = both
+    wide = w_own[...]
+    shared = jnp.where(at_xl == 0, left_left(wide, wide), right_right(wide, wide))
+
+    pulls = [dot_split(grams[p], corners(base[p])) for p in pairs]
+    carried = sum(stat[p] - pulls[p] for p in pairs)
+    shared = shared_pass(shared, both_halves(sum(grams)), both_halves(carried))
+
+    pushed = dot_split(jnp.concatenate(grams, axis=0), corners(shared))
+    state, residual, tables = [], [], []
+    for p in pairs:
+        inverse = ridge_scale(grams[p])
+        rest = stat[p] - pushed[K * p : K * p + K] - RIDGE * pulls[p]
+        state.append(rows_of(base[p]))
+        residual.append(rows_of(rest * inverse))
+        tables.append((RIDGE * grams[p]) * inverse)
+    values = one_pass(state, residual, tables, True)
+    for p in pairs:
+        v_first[p] = values[p]
+
+    later = [grams_next[p] for p in pairs]
+    pulled = dot_split(jnp.concatenate(later, axis=1), jnp.concatenate([corners(v) for v in values], axis=0))
+    carried = sum(stats[p] for p in pairs) - pulled
+    shared = shared_pass(shared, both_halves(sum(later)), both_halves(carried))
+
+    gram, specific = grams_next[at_y], v_first[at_y]
+    inverse = ridge_scale(gram)
+    rest = stats[at_y] - dot_split(gram, corners(shared + RIDGE * specific))
+    (specific,) = one_pass([rows_of(specific)], [rows_of(rest * inverse)], [(RIDGE * gram) * inverse], True)
+    pieces = (left_left(shared, specific), jnp.where(lanes_of(K) < K, shared, specific))
+    for i in range(16):
+        out[i] = pieces[i // 8]
 
 
 def finish_kernel(mine, other, w, v):
@@ -236,8 +295,8 @@
             for i in range(8):
                 at = (8 * half + i) * N
                 wide = min(N, G - at)
-                w[:, at : at + wide] = part[i, :K, :wide]
-                v[0, :, at : at + wide] = part[i, K:, :wide]
+                w[:, at : at + wide] = left_left(part[i], part[8 + i])[:, :wide]
+                v[0, :, at : at + wide] = right_right(part[i], part[8 + i])[:, :wide]
 
     @pl.when(core == 0)
     def _():
@@ -269,29 +328,29 @@
     loads, keep, send, w_own, v_own = pl.pallas_call(
         front_kernel,
         name="front",
-        out_shape=(shape(2, K, N), near(HALF + K, N), near(HALF + K, N), near(K, N), near(K, N)),
+        out_shape=(shape(2, K, N), near(HALF + PACKED, N), near(HALF + PACKED, N), near(K, N), near(K, N)),
         in_specs=[SM, SM, VM, VM, VM, VM],
         out_specs=[VM] * 5,
         scratch_shapes=[pltpu.VMEM((K, K, N), F32)],
     )(dataset_map, sweep_count, expression, picks, shared_init, specific_init)
     came = lax.ppermute(send, "c", SWAP)
     packed = pl.pallas_call(
-        pack_kernel, name="pack", out_shape=near(8, N + K, N), in_specs=[VM, VM], out_specs=VM
+        pack_kernel, name="pack", out_shape=near(8, N + PACKED, N), in_specs=[VM, VM], out_specs=VM
     )(held(keep), held(came))
     came = lax.all_to_all(packed, RING, 0, 0, tiled=True)
     spread = pl.pallas_call(
-        group_kernel, name="group", out_shape=near(8, 2 * N, N), in_specs=[VM, VM], out_specs=VM
+        group_kernel, name="group", out_shape=near(8, K + K // 2 + PACKED, N), in_specs=[VM, VM], out_specs=VM
     )(held(came), held(v_own))
     came = lax.all_to_all(spread, GRP, 0, 0, tiled=True)
     spread = pl.pallas_call(
         update_kernel,
         name="update",
-        out_shape=near(8, N, N),
+        out_shape=near(16, K, N),
         in_specs=[VM, VM],
         out_specs=VM,
-        scratch_shapes=[pltpu.VMEM((8, K, N), F32)],
+        scratch_shapes=[pltpu.VMEM((4, K, N), F32)] * 3,
     )(held(came), held(w_own))
-    mine = lax.all_to_all(spread, RING, 0, 0, tiled=True)
+    mine = lax.all_to_all(spread, PLANE, 0, 0, tiled=True)
     other = lax.ppermute(mine, "c", SWAP)
     shared, specific = pl.pallas_call(
         finish_kernel,

time: 76.6 us -> 68 us (0.89)
  blocking collectives: 52.5 us -> 45.7 us
  Pallas kernels: 14.6 us -> 12.7 us
    all_to_all x1, blocking collectives: 17.5 us -> 12.7 us  [on_device(): came = lax.all_to_all(spread, GRP, 0, 0, tiled=True)]
    pallas_call x3, Pallas kernels: 6.4 us -> 4.28 us  [the longest x1 4.03 us: on_device(): pl.pallas_call(update_kernel, name='update', out_shape=near(16, K, N), in...]
    all_to_all x1, blocking collectives: 14.8 us -> 13.2 us  [on_device(): mine = lax.all_to_all(spread, PLANE, 0, 0, tiled=True)]
where the time goes in v3:
time: 68 us; the launch traced here: 67.7 us
  blocking collectives  45.7 us (67%)
  Pallas kernels  12.7 us (19%)
  starting transfers between devices  5.02 us (7%)
  waiting for transfers between devices  3.1 us (5%)
  between operations  1.29 us (2%)
    all_to_all x1, blocking collectives, on_device(): came = lax.all_to_all(packed, RING, 0, 0, tiled=True)  19.7 us
    all_to_all x1, blocking collectives, on_device(): mine = lax.all_to_all(spread, PLANE, 0, 0, tiled=True)  13.2 us
    all_to_all x1, blocking collectives, on_device(): came = lax.all_to_all(spread, GRP, 0, 0, tiled=True)  12.7 us
    pallas_call x1, Pallas kernels, on_device(): pl.pallas_call(front_kernel, name='front', out_shape=(shape(2, K, N), nea...  7.08 us
    pallas_call x1, Pallas kernels, on_device(): pl.pallas_call(update_kernel, name='update', out_shape=near(16, K, N), in...  4.03 us
    ppermute x1, starting transfers between devices, on_device(): other = lax.ppermute(mine, 'c', SWAP)  3.66 us
    ppermute x1, waiting for transfers between devices, on_device(): came = lax.ppermute(send, 'c', SWAP)  1.57 us
    ppermute x1, waiting for transfers between devices, on_device(): other = lax.ppermute(mine, 'c', SWAP)  1.54 us
  transfers between devices with their start and end apart: 2, of which 2 were waited for; matrix products, arithmetic and copies ran while one was open for 0% of the time, Pallas kernels for 0%

profile of v3, /device:TPU:1, one launch (start us, length us, event | category | flops | bytes accessed | tf_op | source)
XLA Modules:
  0.0 67.7 jit_solution(2683687201152704296)
XLA Ops:
  1.3 7.1 %front.1 = (f32[2,64,128]{2,1,0:T(8,128)}, f32[1064,128]{1,0:T(8,128)S(1)}, f32[1064,128]{1,0:T(8,128)S(1)}, f32[64,128]{1,0:T(8,128)S(1)}, f32[64,128]{1,0:T(8,128)S(1)}) custom-call(s32[1]{0:T(128)S(6)} %copy.9.dmap, s32[8]{0:T(128)} %sweeps.1, bf16[2000,512]{1,0:T(8,128)(2,1)} %x.1, s32[2,128]{1,0:T(2,128)} %picks.1, f32[64,2000]{1,0:T(8,128)} %w.1, ...), custom_call_target="tpu_custom_call" | custom-call | tf_op jit(solution)/shard_map/front/pallas_call | solution.py:328
  8.4 1.4 %collective-permute-start = (f32[1064,128]{1,0:T(8,128)S(1)}, f32[1064,128]{1,0:T(8,128)S(1)}, u32[]{:S(2)}, u32[]{:S(2)}) collective-permute-start(f32[1064,128]{1,0:T(8,128)S(1)} %get-tuple-element.12), channel_id=1, source_target_pairs={{0,1},{1,0},{2,3},{3,2},{4,5},{5,4},{6,7},{7,6},{8,9},{9,8},{10,11... | collective-permute-start | bytes 1634312 | tf_op jit(solution)/shard_map/ppermute | solution.py:336
  9.7 1.6 %collective-permute-done.came = f32[1064,128]{1,0:T(8,128)S(1)} collective-permute-done((f32[1064,128]{1,0:T(8,128)S(1)}, f32[1064,128]{1,0:T(8,128)S(1)}, u32[]{:S(2)}, u32[]{:S(2)}) %collective-permute-start) | collective-permute-done | bytes 544800 | tf_op jit(solution)/shard_map/ppermute | solution.py:336
  11.3 0.1 pack.1
  11.4 19.7 %all_to_all.15.came = f32[8,168,128]{2,1,0:T(8,128)S(1)} all-to-all(f32[8,168,128]{2,1,0:T(8,128)S(1)} %pack.1), channel_id=1, replica_groups=mesh['y'=4,'xl'=2,'xh'=2,'z'=4,'c'=2] {'xh','z'}, dimensions={0} | all-to-all | bytes 1376256 | tf_op jit(solution)/shard_map/all_to_all | solution.py:340
  31.1 0.2 group.1
  31.3 12.7 %all_to_all.16.came = f32[8,136,128]{2,1,0:T(8,128)S(1)} all-to-all(f32[8,136,128]{2,1,0:T(8,128)S(1)} %group.1), channel_id=1, replica_groups=mesh['y'=4,'xl'=2,'xh'=2,'z'=4,'c'=2] {'y','xl'}, dimensions={0} | all-to-all | bytes 1114112 | tf_op jit(solution)/shard_map/all_to_all | solution.py:344
  44.0 4.0 %update.1 = f32[16,64,128]{2,1,0:T(8,128)S(1)} custom-call(f32[8,136,128]{2,1,0:T(8,128)S(1)} %all_to_all.16.came, f32[64,128]{1,0:T(8,128)S(1)} %get-tuple-element.14.w_own), custom_call_target="tpu_custom_call" | custom-call | tf_op jit(solution)/shard_map/update/pallas_call | solution.py:345
  48.1 13.2 %all_to_all.17.mine = f32[16,64,128]{2,1,0:T(8,128)S(1)} all-to-all(f32[16,64,128]{2,1,0:T(8,128)S(1)} %update.1), channel_id=1, replica_groups=mesh['y'=4,'xl'=2,'xh'=2,'z'=4,'c'=2] {'xl','xh','z'}, dimensions={0} | all-to-all | bytes 1048576 | tf_op jit(solution)/shard_map/all_to_all | solution.py:353
  61.2 3.7 %collective-permute-start.1 = (f32[16,64,128]{2,1,0:T(8,128)S(1)}, f32[16,64,128]{2,1,0:T(8,128)S(1)}, u32[]{:S(2)}, u32[]{:S(2)}) collective-permute-start(f32[16,64,128]{2,1,0:T(8,128)S(1)} %all_to_all.17.mine), channel_id=1, source_target_pairs={{0,1},{1,0},{2,3},{3,2},{4,5},{5,4},{6,7},{7,6},{8,9},{9,8},{10,11... | collective-permute-start | bytes 1572872 | tf_op jit(solution)/shard_map/ppermute | solution.py:354
  64.9 1.5 %collective-permute-done.1.other = f32[16,64,128]{2,1,0:T(8,128)S(1)} collective-permute-done((f32[16,64,128]{2,1,0:T(8,128)S(1)}, f32[16,64,128]{2,1,0:T(8,128)S(1)}, u32[]{:S(2)}, u32[]{:S(2)}) %collective-permute-start.1) | collective-permute-done | bytes 524320 | tf_op jit(solution)/shard_map/ppermute | solution.py:354
  66.4 1.3 %finish.1 = (f32[64,2000]{1,0:T(8,128)}, f32[1,64,2000]{2,1,0:T(8,128)}) custom-call(f32[16,64,128]{2,1,0:T(8,128)S(1)} %all_to_all.17.mine, f32[16,64,128]{2,1,0:T(8,128)S(1)} %collective-permute-done.1.other), custom_call_target="tpu_custom_call" | custom-call | tf_op jit(solution)/shard_map/finish/pallas_call | solution.py:355
Async XLA Ops:
  8.4 2.9 %collective-permute-start = (f32[1064,128]{1,0:T(8,128)S(1)}, f32[1064,128]{1,0:T(8,128)S(1)}, u32[]{:S(2)}, u32[]{:S(2)}) collective-permute-start(f32[1064,128]{1,0:T(8,128)S(1)} %get-tuple-element.12), channel_id=1, source_target_pairs={{0,1},{1,0},{2,3},{3,2},{4,5},{5,4},{6,7},{7,6},{8,9},{9,8},{10,11... | collective-permute-start | bytes 1634312 | tf_op jit(solution)/shard_map/ppermute | solution.py:336
  61.2 5.2 %collective-permute-start.1 = (f32[16,64,128]{2,1,0:T(8,128)S(1)}, f32[16,64,128]{2,1,0:T(8,128)S(1)}, u32[]{:S(2)}, u32[]{:S(2)}) collective-permute-start(f32[16,64,128]{2,1,0:T(8,128)S(1)} %all_to_all.17.mine), channel_id=1, source_target_pairs={{0,1},{1,0},{2,3},{3,2},{4,5},{5,4},{6,7},{7,6},{8,9},{9,8},{10,11... | collective-permute-start | bytes 1572872 | tf_op jit(solution)/shard_map/ppermute | solution.py:354

commit v4 on v3

--- a/solution.py
+++ b/solution.py
@@ -39,19 +39,17 @@
     return [x[8 * t : 8 * t + 8] for t in range(K // 8)]
 
 
-def coordinate_steps(state, residual, column):
+def coordinate_steps(state, residual, column, last):
     sub = lax.broadcasted_iota(jnp.int32, (8, N), 0)
     for k in range(K):
         t, s = divmod(k, 8)
-        cols = column(k)
-        for half in range(len(state)):
-            h, r = state[half], residual[half]
+        for half, (h, r) in enumerate(zip(state, residual)):
             change = jnp.maximum(-h[t], r[t])
             spread = jnp.broadcast_to(change[s : s + 1], (8, N))
             h[t] = jnp.where(sub == s, h[t] + change, h[t])
-            for j in range(K // 8):
-                r[j] = r[j] - cols[j] * spread
-    return state
+            for j in range((t if s < 7 else t + 1) if last else 0, K // 8):
+                r[j] = r[j] - column(half, k, j) * spread
+    return [jnp.concatenate(h, axis=0) for h in state]
 
 
 def lanes_of(rows):
@@ -104,27 +102,61 @@
     return first, first + second
 
 
-def front_kernel(dmap, sweeps, x, picks, w, v, loads, keep, send, w_own, v_own, table):
+def split(x):
+    high = x.astype(BF16)
+    return high, (x - high.astype(F32)).astype(BF16)
+
+
+def gram_of(high, low):
+    both = dot_nt(jnp.concatenate([high, low], axis=0), high)
+    return both[:K], both[K:]
+
+
+CHUNK = 512
+
+
+def front_kernel(
+    picks, dmap_hbm, sweeps_hbm, x_hbm, w_hbm, v_hbm,
+    send, cells, state, w_own, v_own,
+    x, w, v, dmap, sweeps, table, sems,
+):
     core = lax.axis_index("c")
     tile = core * 8 + lax.axis_index("xh") * 4 + lax.axis_index("z")
-    count = sweeps[dmap[0]]
-    shared, specific = w[...], v[0]
-    mixed = shared + specific
+    spans = [(at, min(CHUNK, G - at)) for at in range(0, G, CHUNK)]
+    early = [
+        pltpu.make_async_copy(w_hbm, w, sems.at[0]),
+        pltpu.make_async_copy(v_hbm.at[0], v, sems.at[1]),
+        pltpu.make_async_copy(dmap_hbm, dmap, sems.at[2]),
+        pltpu.make_async_copy(sweeps_hbm, sweeps, sems.at[3]),
+    ]
+    parts = [
+        pltpu.make_async_copy(x_hbm.at[pl.ds(at, rows)], x.at[pl.ds(at, rows)], sems.at[4 + i])
+        for i, (at, rows) in enumerate(spans)
+    ]
+    for copy in early + parts:
+        copy.start()
+    early[0].wait()
+    early[1].wait()
 
     @pl.when(tile < 15)
     def _():
         at = pl.multiple_of(jnp.minimum(tile, 14) * N, N)
         w_own[...] = w[:, pl.ds(at, N)]
-        v_own[...] = v[0, :, pl.ds(at, N)]
+        v_own[...] = v[:, pl.ds(at, N)]
 
     @pl.when(tile == 15)
     def _():
         w_own[...] = jnp.zeros((K, N), F32)
         v_own[...] = jnp.zeros((K, N), F32)
         w_own[:, :LAST] = w[:, 15 * N :]
-        v_own[:, :LAST] = v[0, :, 15 * N :]
-
-    gram = dot_nt(mixed, mixed, HIGHEST) + LAMBDA * dot_nt(specific, specific, HIGHEST)
+        v_own[:, :LAST] = v[:, 15 * N :]
+
+    specific = v[...]
+    mixed_high, mixed_low = split(w[...] + specific)
+    mixed_gram, mixed_cross = gram_of(mixed_high, mixed_low)
+    own_gram, own_cross = gram_of(*split(specific))
+    cross = mixed_cross + LAMBDA * own_cross
+    gram = mixed_gram + LAMBDA * own_gram + cross + cross.T
     inverse = 1.0 / (diagonal(gram) + EPSILON)
     scaled = gram * inverse
     for k in range(K):
@@ -134,49 +166,50 @@
     choose = jnp.concatenate(
         [(pool == picks[r : r + 1, :]).astype(F32).astype(BF16) for r in range(2)], axis=1
     )
-    cells = jnp.dot(x[...], choose, preferred_element_type=F32).astype(BF16)
-    target = jnp.dot(mixed.astype(BF16), cells, preferred_element_type=F32) * inverse
+    for copy, (at, rows) in zip(parts, spans):
+        copy.wait()
+        part = jnp.dot(x[at : at + rows], choose, preferred_element_type=F32)
+        cells[at : at + rows] = part.astype(BF16)
+    cells[G:] = jnp.zeros((2 * HALF - G, 2 * N), BF16)
+    target = jnp.dot(mixed_high, cells[:G], preferred_element_type=F32) * inverse
+    early[2].wait()
+    early[3].wait()
+    count = sweeps[dmap[0]]
+
+    def column(_, k, j):
+        return table[k, 8 * j : 8 * j + 8]
 
     def sweep(_, carry):
-        state = [list(carry[0]), list(carry[1])]
-        residual = [list(carry[2]), list(carry[3])]
-        coordinate_steps(state, residual, lambda k: [table[k, 8 * j : 8 * j + 8] for j in range(K // 8)])
-        return (tuple(state[0]), tuple(state[1]), tuple(residual[0]), tuple(residual[1]))
+        parts = [list(part) for part in carry]
+        coordinate_steps(parts[:2], parts[2:], column, False)
+        return tuple(tuple(part) for part in parts)
 
     none = tuple(jnp.zeros((8, N), F32) for _ in range(K // 8))
     carry = (none, none, tuple(rows_of(target[:, :N])), tuple(rows_of(target[:, N:])))
-    carry = lax.fori_loop(0, count, sweep, carry)
-    first = jnp.concatenate(carry[0], axis=0)
-    second = jnp.concatenate(carry[1], axis=0)
-    loads[0] = first
-    loads[1] = second
+    parts = [list(part) for part in lax.fori_loop(0, count - 1, sweep, carry)]
+    first, second = coordinate_steps(parts[:2], parts[2:], column, True)
     zero = jnp.zeros((K, N), F32)
     both = jnp.concatenate([first, second], axis=1)
     block = jnp.concatenate(
         [jnp.concatenate([first, zero], axis=1), jnp.concatenate([zero, second], axis=1)], axis=0
     )
-    gram_part = fold_grams(dot_nt(both, block, HIGHEST))
-    keep[HALF:] = gram_part
-    send[HALF:] = gram_part
-    rounded = block.astype(BF16)
-    low = dot_nt(cells[:HALF], rounded)
-    high = dot_nt(cells[HALF:], rounded)
-
-    @pl.when(core == 0)
-    def _():
-        keep[:HALF] = low
-        send[: G - HALF] = high
-        send[G - HALF : HALF] = jnp.zeros((2 * HALF - G, N), F32)
-
-    @pl.when(core == 1)
-    def _():
-        send[:HALF] = low
-        keep[: G - HALF] = high
-        keep[G - HALF : HALF] = jnp.zeros((2 * HALF - G, N), F32)
-
-
-def pack_kernel(keep, came, out):
-    gram = keep[HALF:] + came[HALF:]
+    state[...] = block
+    away = pl.multiple_of((1 - core) * HALF, HALF)
+    send[:HALF] = dot_nt(cells[pl.ds(away, HALF)], block.astype(BF16))
+    send[HALF:] = fold_grams(dot_nt(both, block, HIGHEST))
+
+
+def keep_kernel(cells, state, keep, loads):
+    core = lax.axis_index("c")
+    home = pl.multiple_of(core * HALF, HALF)
+    block = state[...]
+    loads[0] = block[:K, :N]
+    loads[1] = block[K:, N:]
+    keep[...] = dot_nt(cells[pl.ds(home, HALF)], block.astype(BF16))
+
+
+def pack_kernel(keep, send, came, out):
+    gram = send[HALF:] + came[HALF:]
     for i in range(8):
         out[i, :N] = keep[N * i : N * i + N] + came[N * i : N * i + N]
         out[i, N:] = gram
@@ -320,31 +353,60 @@
 
 
 VM = pl.BlockSpec(memory_space=pltpu.VMEM)
-SM = pl.BlockSpec(memory_space=pltpu.SMEM)
+FAR = pl.BlockSpec(memory_space=pltpu.HBM)
 SWAP = [(0, 1), (1, 0)]
+LIMIT = pltpu.CompilerParams(vmem_limit_bytes=24 << 20)
 
 
 def on_device(expression, dataset_id, dataset_map, sweep_count, picks, shared_init, specific_init):
-    loads, keep, send, w_own, v_own = pl.pallas_call(
+    send, cells, state, w_own, v_own = pl.pallas_call(
         front_kernel,
         name="front",
-        out_shape=(shape(2, K, N), near(HALF + PACKED, N), near(HALF + PACKED, N), near(K, N), near(K, N)),
-        in_specs=[SM, SM, VM, VM, VM, VM],
+        out_shape=(
+            near(HALF + PACKED, N),
+            pltpu.VMEM((2 * HALF, 2 * N), BF16),
+            near(N, 2 * N),
+            near(K, N),
+            near(K, N),
+        ),
+        in_specs=[VM] + [FAR] * 5,
         out_specs=[VM] * 5,
-        scratch_shapes=[pltpu.VMEM((K, K, N), F32)],
-    )(dataset_map, sweep_count, expression, picks, shared_init, specific_init)
+        scratch_shapes=[
+            pltpu.VMEM((G, expression.shape[1]), BF16),
+            pltpu.VMEM((K, G), F32),
+            pltpu.VMEM((K, G), F32),
+            pltpu.SMEM(dataset_map.shape, jnp.int32),
+            pltpu.SMEM(sweep_count.shape, jnp.int32),
+            pltpu.VMEM((K, K, N), F32),
+            pltpu.SemaphoreType.DMA((8,)),
+        ],
+    )(picks, dataset_map, sweep_count, expression, shared_init, specific_init)
     came = lax.ppermute(send, "c", SWAP)
+    keep, loads = pl.pallas_call(
+        keep_kernel,
+        name="keep",
+        compiler_params=LIMIT,
+        out_shape=(near(HALF, N), shape(2, K, N)),
+        in_specs=[VM, VM],
+        out_specs=[VM, VM],
+    )(held(cells), held(state))
     packed = pl.pallas_call(
-        pack_kernel, name="pack", out_shape=near(8, N + PACKED, N), in_specs=[VM, VM], out_specs=VM
-    )(held(keep), held(came))
+        pack_kernel,
+        name="pack",
+        compiler_params=LIMIT,
+        out_shape=near(8, N + PACKED, N),
+        in_specs=[VM] * 3,
+        out_specs=VM,
+    )(held(keep), held(send), held(came))
     came = lax.all_to_all(packed, RING, 0, 0, tiled=True)
     spread = pl.pallas_call(
-        group_kernel, name="group", out_shape=near(8, K + K // 2 + PACKED, N), in_specs=[VM, VM], out_specs=VM
+        group_kernel, name="group", compiler_params=LIMIT, out_shape=near(8, K + K // 2 + PACKED, N), in_specs=[VM, VM], out_specs=VM
     )(held(came), held(v_own))
     came = lax.all_to_all(spread, GRP, 0, 0, tiled=True)
     spread = pl.pallas_call(
         update_kernel,
         name="update",
+        compiler_params=LIMIT,
         out_shape=near(16, K, N),
         in_specs=[VM, VM],
         out_specs=VM,
@@ -355,6 +417,7 @@
     shared, specific = pl.pallas_call(
         finish_kernel,
         name="finish",
+        compiler_params=LIMIT,
         out_shape=(shape(K, G), shape(1, K, G)),
         in_specs=[VM, VM],
         out_specs=[VM, VM],

time: 68 us -> 68.2 us (level)
  Pallas kernels: 12.7 us -> 13.8 us
  waiting for transfers between devices: 3.1 us -> 2.32 us
    pallas_call x5 -> x6, Pallas kernels: 12.7 us -> 13.8 us  [the longest x1 7.47 us: on_device(): pl.pallas_call(front_kernel, name='front', out_shape=(near(HALF + PACKED,...]
    ppermute x1, waiting for transfers between devices: 1.57 us -> 0.78 us  [on_device(): came = lax.ppermute(send, 'c', SWAP)]
  transfers between devices with their start and end apart: 2 -> 2, of which waited for: 2 -> 2; matrix products, arithmetic and copies ran while one was open for 0% -> 0% of each run, Pallas kernels for 0% -> 1%
where the time goes in v4:
time: 68.2 us; the launch traced here: 68 us
  blocking collectives  45.4 us (67%)
  Pallas kernels  13.8 us (20%)
  starting transfers between devices  5.13 us (8%)
  waiting for transfers between devices  2.32 us (3%)
  between operations  1.3 us (2%)
    all_to_all x1, blocking collectives, on_device(): came = lax.all_to_all(packed, RING, 0, 0, tiled=True)  19.7 us
    all_to_all x1, blocking collectives, on_device(): mine = lax.all_to_all(spread, PLANE, 0, 0, tiled=True)  13.3 us
    all_to_all x1, blocking collectives, on_device(): came = lax.all_to_all(spread, GRP, 0, 0, tiled=True)  12.3 us
    pallas_call x1, Pallas kernels, on_device(): pl.pallas_call(front_kernel, name='front', out_shape=(near(HALF + PACKED,...  7.47 us
    pallas_call x1, Pallas kernels, on_device(): pl.pallas_call(update_kernel, name='update', compiler_params=LIMIT, out_s...  4.03 us
    ppermute x1, starting transfers between devices, on_device(): other = lax.ppermute(mine, 'c', SWAP)  3.66 us
    ppermute x1, waiting for transfers between devices, on_device(): other = lax.ppermute(mine, 'c', SWAP)  1.54 us
    ppermute x1, starting transfers between devices, on_device(): came = lax.ppermute(send, 'c', SWAP)  1.46 us
  transfers between devices with their start and end apart: 2, of which 2 were waited for; matrix products, arithmetic and copies ran while one was open for 0% of the time, Pallas kernels for 1%

profile of v4, /device:TPU:1, one launch (start us, length us, event | category | flops | bytes accessed | tf_op | source)
XLA Modules:
  0.0 68.0 jit_solution(17268803200378802870)
XLA Ops:
  1.3 7.5 %front.1 = (f32[1064,128]{1,0:T(8,128)S(1)}, bf16[2048,256]{1,0:T(8,128)(2,1)S(1)}, f32[128,256]{1,0:T(8,128)S(1)}, f32[64,128]{1,0:T(8,128)S(1)}, f32[64,128]{1,0:T(8,128)S(1)}) custom-call(s32[2,128]{1,0:T(2,128)} %picks.1, s32[1]{0:T(128)S(6)} %copy.9.dmap_hbm, s32[8]{0:T(128)} %sweeps_hbm.1, bf16[2000,512]{1,0:T(8,128)(2,1)} %x_hbm.1, f32[64,2000]{1,0:T(8,128)} %w_hbm.1, ...), custom_call_target="tpu_custom_call" | custom-call | tf_op jit(solution)/shard_map/front/pallas_call | solution.py:362
  8.8 1.5 %collective-permute-start = (f32[1064,128]{1,0:T(8,128)S(1)}, f32[1064,128]{1,0:T(8,128)S(1)}, u32[]{:S(2)}, u32[]{:S(2)}) collective-permute-start(f32[1064,128]{1,0:T(8,128)S(1)} %get-tuple-element.16.send), channel_id=1, source_target_pairs={{0,1},{1,0},{2,3},{3,2},{4,5},{5,4},{6,7},{7,6},{8,9},{9,8},{10,11... | collective-permute-start | bytes 1634312 | tf_op jit(solution)/shard_map/ppermute | solution.py:384
  10.2 0.8 %keep.1 = (f32[1024,128]{1,0:T(8,128)S(1)}, f32[2,64,128]{2,1,0:T(8,128)}) custom-call(bf16[2048,256]{1,0:T(8,128)(2,1)S(1)} %get-tuple-element.12.cells, f32[128,256]{1,0:T(8,128)S(1)} %get-tuple-element.13.state), custom_call_target="tpu_custom_call" | custom-call | tf_op jit(solution)/shard_map/keep/pallas_call | solution.py:385
  11.0 0.8 %collective-permute-done.came = f32[1064,128]{1,0:T(8,128)S(1)} collective-permute-done((f32[1064,128]{1,0:T(8,128)S(1)}, f32[1064,128]{1,0:T(8,128)S(1)}, u32[]{:S(2)}, u32[]{:S(2)}) %collective-permute-start) | collective-permute-done | bytes 544800 | tf_op jit(solution)/shard_map/ppermute | solution.py:384
  11.8 0.1 pack.1
  11.9 19.7 %all_to_all.15.came = f32[8,168,128]{2,1,0:T(8,128)S(1)} all-to-all(f32[8,168,128]{2,1,0:T(8,128)S(1)} %pack.1), channel_id=1, replica_groups=mesh['y'=4,'xl'=2,'xh'=2,'z'=4,'c'=2] {'xh','z'}, dimensions={0} | all-to-all | bytes 1376256 | tf_op jit(solution)/shard_map/all_to_all | solution.py:401
  31.6 0.2 group.1
  31.8 12.3 %all_to_all.16.came = f32[8,136,128]{2,1,0:T(8,128)S(1)} all-to-all(f32[8,136,128]{2,1,0:T(8,128)S(1)} %group.1), channel_id=1, replica_groups=mesh['y'=4,'xl'=2,'xh'=2,'z'=4,'c'=2] {'y','xl'}, dimensions={0} | all-to-all | bytes 1114112 | tf_op jit(solution)/shard_map/all_to_all | solution.py:405
  44.1 4.0 %update.1 = f32[16,64,128]{2,1,0:T(8,128)S(1)} custom-call(f32[8,136,128]{2,1,0:T(8,128)S(1)} %all_to_all.16.came, f32[64,128]{1,0:T(8,128)S(1)} %get-tuple-element.18.w_own), custom_call_target="tpu_custom_call" | custom-call | tf_op jit(solution)/shard_map/update/pallas_call | solution.py:406
  48.1 13.3 %all_to_all.17.mine = f32[16,64,128]{2,1,0:T(8,128)S(1)} all-to-all(f32[16,64,128]{2,1,0:T(8,128)S(1)} %update.1), channel_id=1, replica_groups=mesh['y'=4,'xl'=2,'xh'=2,'z'=4,'c'=2] {'xl','xh','z'}, dimensions={0} | all-to-all | bytes 1048576 | tf_op jit(solution)/shard_map/all_to_all | solution.py:415
  61.5 3.7 %collective-permute-start.1 = (f32[16,64,128]{2,1,0:T(8,128)S(1)}, f32[16,64,128]{2,1,0:T(8,128)S(1)}, u32[]{:S(2)}, u32[]{:S(2)}) collective-permute-start(f32[16,64,128]{2,1,0:T(8,128)S(1)} %all_to_all.17.mine), channel_id=1, source_target_pairs={{0,1},{1,0},{2,3},{3,2},{4,5},{5,4},{6,7},{7,6},{8,9},{9,8},{10,11... | collective-permute-start | bytes 1572872 | tf_op jit(solution)/shard_map/ppermute | solution.py:416
  65.1 1.5 %collective-permute-done.1.other = f32[16,64,128]{2,1,0:T(8,128)S(1)} collective-permute-done((f32[16,64,128]{2,1,0:T(8,128)S(1)}, f32[16,64,128]{2,1,0:T(8,128)S(1)}, u32[]{:S(2)}, u32[]{:S(2)}) %collective-permute-start.1) | collective-permute-done | bytes 524320 | tf_op jit(solution)/shard_map/ppermute | solution.py:416
  66.7 1.3 %finish.1 = (f32[64,2000]{1,0:T(8,128)}, f32[1,64,2000]{2,1,0:T(8,128)}) custom-call(f32[16,64,128]{2,1,0:T(8,128)S(1)} %all_to_all.17.mine, f32[16,64,128]{2,1,0:T(8,128)S(1)} %collective-permute-done.1.other), custom_call_target="tpu_custom_call" | custom-call | tf_op jit(solution)/shard_map/finish/pallas_call | solution.py:417
Async XLA Ops:
  8.8 3.0 %collective-permute-start = (f32[1064,128]{1,0:T(8,128)S(1)}, f32[1064,128]{1,0:T(8,128)S(1)}, u32[]{:S(2)}, u32[]{:S(2)}) collective-permute-start(f32[1064,128]{1,0:T(8,128)S(1)} %get-tuple-element.16.send), channel_id=1, source_target_pairs={{0,1},{1,0},{2,3},{3,2},{4,5},{5,4},{6,7},{7,6},{8,9},{9,8},{10,11... | collective-permute-start | bytes 1634312 | tf_op jit(solution)/shard_map/ppermute | solution.py:384
  61.5 5.2 %collective-permute-start.1 = (f32[16,64,128]{2,1,0:T(8,128)S(1)}, f32[16,64,128]{2,1,0:T(8,128)S(1)}, u32[]{:S(2)}, u32[]{:S(2)}) collective-permute-start(f32[16,64,128]{2,1,0:T(8,128)S(1)} %all_to_all.17.mine), channel_id=1, source_target_pairs={{0,1},{1,0},{2,3},{3,2},{4,5},{5,4},{6,7},{7,6},{8,9},{9,8},{10,11... | collective-permute-start | bytes 1572872 | tf_op jit(solution)/shard_map/ppermute | solution.py:416

commit v5 on v4

--- a/solution.py
+++ b/solution.py
@@ -112,31 +112,35 @@
     return both[:K], both[K:]
 
 
-CHUNK = 512
-
-
 def front_kernel(
-    picks, dmap_hbm, sweeps_hbm, x_hbm, w_hbm, v_hbm,
+    picks_hbm, ids_hbm, sweeps_hbm, x_hbm, w_hbm, v_hbm,
     send, cells, state, w_own, v_own,
-    x, w, v, dmap, sweeps, table, sems,
+    picks, ids, sweeps, x, w, v, choose, table, sems,
 ):
     core = lax.axis_index("c")
     tile = core * 8 + lax.axis_index("xh") * 4 + lax.axis_index("z")
-    spans = [(at, min(CHUNK, G - at)) for at in range(0, G, CHUNK)]
-    early = [
-        pltpu.make_async_copy(w_hbm, w, sems.at[0]),
-        pltpu.make_async_copy(v_hbm.at[0], v, sems.at[1]),
-        pltpu.make_async_copy(dmap_hbm, dmap, sems.at[2]),
-        pltpu.make_async_copy(sweeps_hbm, sweeps, sems.at[3]),
+    copies = [
+        pltpu.make_async_copy(source, target, sems.at[i])
+        for i, (source, target) in enumerate(
+            [
+                (picks_hbm, picks),
+                (w_hbm, w),
+                (v_hbm.at[0], v),
+                (x_hbm, x),
+                (ids_hbm, ids),
+                (sweeps_hbm, sweeps),
+            ]
+        )
     ]
-    parts = [
-        pltpu.make_async_copy(x_hbm.at[pl.ds(at, rows)], x.at[pl.ds(at, rows)], sems.at[4 + i])
-        for i, (at, rows) in enumerate(spans)
-    ]
-    for copy in early + parts:
+    for copy in copies:
         copy.start()
-    early[0].wait()
-    early[1].wait()
+    copies[0].wait()
+    pool = lax.broadcasted_iota(jnp.int32, (x.shape[1], N), 0)
+    for r in range(2):
+        choose[:, N * r : N * r + N] = (pool == picks[r : r + 1, :]).astype(F32).astype(BF16)
+    cells[G:] = jnp.zeros((2 * HALF - G, 2 * N), BF16)
+    copies[1].wait()
+    copies[2].wait()
 
     @pl.when(tile < 15)
     def _():
@@ -159,22 +163,13 @@
     gram = mixed_gram + LAMBDA * own_gram + cross + cross.T
     inverse = 1.0 / (diagonal(gram) + EPSILON)
     scaled = gram * inverse
+    for copy in copies[3:]:
+        copy.wait()
+    cells[:G] = jnp.dot(x[...], choose[...], preferred_element_type=F32).astype(BF16)
     for k in range(K):
         table[k] = jnp.broadcast_to(scaled[:, k : k + 1], (K, N))
-
-    pool = lax.broadcasted_iota(jnp.int32, (x.shape[1], N), 0)
-    choose = jnp.concatenate(
-        [(pool == picks[r : r + 1, :]).astype(F32).astype(BF16) for r in range(2)], axis=1
-    )
-    for copy, (at, rows) in zip(parts, spans):
-        copy.wait()
-        part = jnp.dot(x[at : at + rows], choose, preferred_element_type=F32)
-        cells[at : at + rows] = part.astype(BF16)
-    cells[G:] = jnp.zeros((2 * HALF - G, 2 * N), BF16)
     target = jnp.dot(mixed_high, cells[:G], preferred_element_type=F32) * inverse
-    early[2].wait()
-    early[3].wait()
-    count = sweeps[dmap[0]]
+    count = sweeps[ids[0]]
 
     def column(_, k, j):
         return table[k, 8 * j : 8 * j + 8]
@@ -320,24 +315,27 @@
         out[i] = pieces[i // 8]
 
 
-def finish_kernel(mine, other, w, v):
-    core = lax.axis_index("c")
-
-    def write(first, second):
-        for half, part in enumerate((first, second)):
-            for i in range(8):
-                at = (8 * half + i) * N
-                wide = min(N, G - at)
-                w[:, at : at + wide] = left_left(part[i], part[8 + i])[:, :wide]
-                v[0, :, at : at + wide] = right_right(part[i], part[8 + i])[:, :wide]
-
-    @pl.when(core == 0)
-    def _():
-        write(mine, other)
-
-    @pl.when(core == 1)
-    def _():
-        write(other, mine)
+def finish_kernel(part, *refs):
+    w, v = refs[-2:]
+    for i in range(8):
+        w[:, N * i : N * i + N] = left_left(part[i], part[8 + i])
+        v[0, :, N * i : N * i + N] = right_right(part[i], part[8 + i])
+
+
+def finish(part, half, name, earlier=()):
+    return pl.pallas_call(
+        finish_kernel,
+        name=name,
+        compiler_params=LIMIT,
+        grid=(1,),
+        out_shape=(shape(K, G), shape(1, K, G)),
+        in_specs=[VM] + [FAR] * len(earlier),
+        out_specs=[
+            pl.BlockSpec((K, HALF), lambda i: (0, half())),
+            pl.BlockSpec((1, K, HALF), lambda i: (0, 0, half())),
+        ],
+        input_output_aliases={1: 0, 2: 1} if earlier else {},
+    )(held(part), *earlier)
 
 
 def shape(*dims):
@@ -369,18 +367,20 @@
             near(K, N),
             near(K, N),
         ),
-        in_specs=[VM] + [FAR] * 5,
+        in_specs=[FAR] * 6,
         out_specs=[VM] * 5,
         scratch_shapes=[
-            pltpu.VMEM((G, expression.shape[1]), BF16),
-            pltpu.VMEM((K, G), F32),
-            pltpu.VMEM((K, G), F32),
-            pltpu.SMEM(dataset_map.shape, jnp.int32),
+            pltpu.VMEM(picks.shape, jnp.int32),
+            pltpu.SMEM(dataset_id.shape, jnp.int32),
             pltpu.SMEM(sweep_count.shape, jnp.int32),
+            pltpu.VMEM(expression.shape, BF16),
+            pltpu.VMEM(shared_init.shape, F32),
+            pltpu.VMEM(shared_init.shape, F32),
+            pltpu.VMEM((expression.shape[1], 2 * N), BF16),
             pltpu.VMEM((K, K, N), F32),
-            pltpu.SemaphoreType.DMA((8,)),
+            pltpu.SemaphoreType.DMA((6,)),
         ],
-    )(picks, dataset_map, sweep_count, expression, shared_init, specific_init)
+    )(picks, dataset_id, sweep_count, expression, shared_init, specific_init)
     came = lax.ppermute(send, "c", SWAP)
     keep, loads = pl.pallas_call(
         keep_kernel,
@@ -414,14 +414,8 @@
     )(held(came), held(w_own))
     mine = lax.all_to_all(spread, PLANE, 0, 0, tiled=True)
     other = lax.ppermute(mine, "c", SWAP)
-    shared, specific = pl.pallas_call(
-        finish_kernel,
-        name="finish",
-        compiler_params=LIMIT,
-        out_shape=(shape(K, G), shape(1, K, G)),
-        in_specs=[VM, VM],
-        out_specs=[VM, VM],
-    )(held(mine), held(other))
+    bases = finish(mine, lambda: lax.axis_index("c"), "mine")
+    shared, specific = finish(other, lambda: 1 - lax.axis_index("c"), "other", bases)
     return loads, shared, specific
 
 

time: 68.2 us -> 65.5 us (0.960)
  Pallas kernels: 13.8 us -> 11.9 us
  waiting for transfers between devices: 2.32 us -> 1.34 us
  blocking collectives: 45.4 us -> 46.1 us
    pallas_call x1, Pallas kernels: 7.47 us -> 4.91 us  [on_device(): pl.pallas_call(front_kernel, name='front', out_shape=(near(HALF + PACKED,...]
    ppermute x1, waiting for transfers between devices: 1.54 us -> 0.55 us  [on_device(): other = lax.ppermute(mine, 'c', SWAP)]
    all_to_all x1, blocking collectives: 12.3 us -> 13 us  [on_device(): came = lax.all_to_all(spread, GRP, 0, 0, tiled=True)]
    pallas_call x1 -> x2, Pallas kernels: 1.3 us -> 1.96 us  [finish(): pl.pallas_call(finish_kernel, name=name, compiler_params=LIMIT, grid=(1,)...]
  transfers between devices with their start and end apart: 2 -> 2, of which waited for: 2 -> 2; matrix products, arithmetic and copies ran while one was open for 0% -> 0% of each run, Pallas kernels for 1% -> 3%
where the time goes in v5:
time: 65.5 us; the launch traced here: 65.2 us
  blocking collectives  46.1 us (70%)
  Pallas kernels  11.9 us (18%)
  starting transfers between devices  5.12 us (8%)
  waiting for transfers between devices  1.34 us (2%)
    all_to_all x1, blocking collectives, on_device(): came = lax.all_to_all(packed, RING, 0, 0, tiled=True)  19.7 us
    all_to_all x1, blocking collectives, on_device(): mine = lax.all_to_all(spread, PLANE, 0, 0, tiled=True)  13.3 us
    all_to_all x1, blocking collectives, on_device(): came = lax.all_to_all(spread, GRP, 0, 0, tiled=True)  13 us
    pallas_call x1, Pallas kernels, on_device(): pl.pallas_call(front_kernel, name='front', out_shape=(near(HALF + PACKED,...  4.91 us
    pallas_call x1, Pallas kernels, on_device(): pl.pallas_call(update_kernel, name='update', compiler_params=LIMIT, out_s...  4.03 us
    ppermute x1, starting transfers between devices, on_device(): other = lax.ppermute(mine, 'c', SWAP)  3.66 us
    pallas_call x2, Pallas kernels, finish(): pl.pallas_call(finish_kernel, name=name, compiler_params=LIMIT, grid=(1,)...  1.96 us
    ppermute x1, starting transfers between devices, on_device(): came = lax.ppermute(send, 'c', SWAP)  1.46 us
  transfers between devices with their start and end apart: 2, of which 2 were waited for; matrix products, arithmetic and copies ran while one was open for 0% of the time, Pallas kernels for 3%

profile of v5, /device:TPU:1, one launch (start us, length us, event | category | flops | bytes accessed | tf_op | source)
XLA Modules:
  0.0 65.2 jit_solution(9117051497681389849)
XLA Ops:
  0.6 4.9 %front.1 = (f32[1064,128]{1,0:T(8,128)S(1)}, bf16[2048,256]{1,0:T(8,128)(2,1)S(1)}, f32[128,256]{1,0:T(8,128)S(1)}, f32[64,128]{1,0:T(8,128)S(1)}, f32[64,128]{1,0:T(8,128)S(1)}) custom-call(s32[2,128]{1,0:T(2,128)} %picks_hbm.1, s32[512]{0:T(512)} %ids_hbm.1, s32[8]{0:T(128)} %sweeps_hbm.1, bf16[2000,512]{1,0:T(8,128)(2,1)} %x_hbm.1, f32[64,2000]{1,0:T(8,128)} %w_hbm.1, ...), custom_call_target="tpu_custom_call" | custom-call | tf_op jit(solution)/shard_map/front/pallas_call | solution.py:360
  5.6 1.5 %collective-permute-start = (f32[1064,128]{1,0:T(8,128)S(1)}, f32[1064,128]{1,0:T(8,128)S(1)}, u32[]{:S(2)}, u32[]{:S(2)}) collective-permute-start(f32[1064,128]{1,0:T(8,128)S(1)} %get-tuple-element.18.send), channel_id=1, source_target_pairs={{0,1},{1,0},{2,3},{3,2},{4,5},{5,4},{6,7},{7,6},{8,9},{9,8},{10,11... | collective-permute-start | bytes 1634312 | tf_op jit(solution)/shard_map/ppermute | solution.py:384
  7.0 0.8 %keep.1 = (f32[1024,128]{1,0:T(8,128)S(1)}, f32[2,64,128]{2,1,0:T(8,128)}) custom-call(bf16[2048,256]{1,0:T(8,128)(2,1)S(1)} %get-tuple-element.14.cells, f32[128,256]{1,0:T(8,128)S(1)} %get-tuple-element.15.state), custom_call_target="tpu_custom_call" | custom-call | tf_op jit(solution)/shard_map/keep/pallas_call | solution.py:385
  7.8 0.8 %collective-permute-done.came = f32[1064,128]{1,0:T(8,128)S(1)} collective-permute-done((f32[1064,128]{1,0:T(8,128)S(1)}, f32[1064,128]{1,0:T(8,128)S(1)}, u32[]{:S(2)}, u32[]{:S(2)}) %collective-permute-start) | collective-permute-done | bytes 544800 | tf_op jit(solution)/shard_map/ppermute | solution.py:384
  8.6 0.1 pack.1
  8.7 19.7 %all_to_all.15.came = f32[8,168,128]{2,1,0:T(8,128)S(1)} all-to-all(f32[8,168,128]{2,1,0:T(8,128)S(1)} %pack.1), channel_id=1, replica_groups=mesh['y'=4,'xl'=2,'xh'=2,'z'=4,'c'=2] {'xh','z'}, dimensions={0} | all-to-all | bytes 1376256 | tf_op jit(solution)/shard_map/all_to_all | solution.py:401
  28.4 0.2 group.1
  28.6 13.0 %all_to_all.16.came = f32[8,136,128]{2,1,0:T(8,128)S(1)} all-to-all(f32[8,136,128]{2,1,0:T(8,128)S(1)} %group.1), channel_id=1, replica_groups=mesh['y'=4,'xl'=2,'xh'=2,'z'=4,'c'=2] {'y','xl'}, dimensions={0} | all-to-all | bytes 1114112 | tf_op jit(solution)/shard_map/all_to_all | solution.py:405
  41.6 4.0 %update.1 = f32[16,64,128]{2,1,0:T(8,128)S(1)} custom-call(f32[8,136,128]{2,1,0:T(8,128)S(1)} %all_to_all.16.came, f32[64,128]{1,0:T(8,128)S(1)} %get-tuple-element.20.w_own), custom_call_target="tpu_custom_call" | custom-call | tf_op jit(solution)/shard_map/update/pallas_call | solution.py:406
  45.7 13.3 %all_to_all.17.part = f32[16,64,128]{2,1,0:T(8,128)S(1)} all-to-all(f32[16,64,128]{2,1,0:T(8,128)S(1)} %update.1), channel_id=1, replica_groups=mesh['y'=4,'xl'=2,'xh'=2,'z'=4,'c'=2] {'xl','xh','z'}, dimensions={0} | all-to-all | bytes 1048576 | tf_op jit(solution)/shard_map/all_to_all | solution.py:415
  59.0 3.7 %collective-permute-start.1 = (f32[16,64,128]{2,1,0:T(8,128)S(1)}, f32[16,64,128]{2,1,0:T(8,128)S(1)}, u32[]{:S(2)}, u32[]{:S(2)}) collective-permute-start(f32[16,64,128]{2,1,0:T(8,128)S(1)} %all_to_all.17.part), channel_id=1, source_target_pairs={{0,1},{1,0},{2,3},{3,2},{4,5},{5,4},{6,7},{7,6},{8,9},{9,8},{10,11... | collective-permute-start | bytes 1572872 | tf_op jit(solution)/shard_map/ppermute | solution.py:416
  62.6 1.0 %mine.1 = (f32[64,2000]{1,0:T(8,128)}, f32[1,64,2000]{2,1,0:T(8,128)}) custom-call(f32[16,64,128]{2,1,0:T(8,128)S(1)} %all_to_all.17.part), custom_call_target="tpu_custom_call" | custom-call | tf_op jit(solution)/shard_map/mine/pallas_call | solution.py:326
  63.6 0.6 collective-permute-done.1.part
  64.2 1.0 %other.1 = (f32[64,2000]{1,0:T(8,128)}, f32[1,64,2000]{2,1,0:T(8,128)}) custom-call(f32[16,64,128]{2,1,0:T(8,128)S(1)} %collective-permute-done.1.part, f32[64,2000]{1,0:T(8,128)} %get-tuple-element.21.refs_0_, f32[1,64,2000]{2,1,0:T(8,128)} %get-tuple-element.22.refs_1_), custom_call_target="tpu_custom_call", output_to_operand_aliasing={{0}: (1, {}), {1}: (2, {})} | custom-call | tf_op jit(solution)/shard_map/other/pallas_call | solution.py:326
Async XLA Ops:
  5.6 3.0 %collective-permute-start = (f32[1064,128]{1,0:T(8,128)S(1)}, f32[1064,128]{1,0:T(8,128)S(1)}, u32[]{:S(2)}, u32[]{:S(2)}) collective-permute-start(f32[1064,128]{1,0:T(8,128)S(1)} %get-tuple-element.18.send), channel_id=1, source_target_pairs={{0,1},{1,0},{2,3},{3,2},{4,5},{5,4},{6,7},{7,6},{8,9},{9,8},{10,11... | collective-permute-start | bytes 1634312 | tf_op jit(solution)/shard_map/ppermute | solution.py:384
  59.0 5.2 %collective-permute-start.1 = (f32[16,64,128]{2,1,0:T(8,128)S(1)}, f32[16,64,128]{2,1,0:T(8,128)S(1)}, u32[]{:S(2)}, u32[]{:S(2)}) collective-permute-start(f32[16,64,128]{2,1,0:T(8,128)S(1)} %all_to_all.17.part), channel_id=1, source_target_pairs={{0,1},{1,0},{2,3},{3,2},{4,5},{5,4},{6,7},{7,6},{8,9},{9,8},{10,11... | collective-permute-start | bytes 1572872 | tf_op jit(solution)/shard_map/ppermute | solution.py:416

commit v6 on v5

--- a/solution.py
+++ b/solution.py
@@ -194,7 +194,11 @@
     send[HALF:] = fold_grams(dot_nt(both, block, HIGHEST))
 
 
-def keep_kernel(cells, state, keep, loads):
+def keep_kernel(cells, state, keep, loads, spread):
+    rows = lax.broadcasted_iota(jnp.int32, (2 * N, N), 0) % N
+    at = rows - jnp.where(lanes_of(2 * N) < K, 0, K)
+    for k in range(K):
+        spread[:, N * k : N * k + N] = (at == k).astype(F32).astype(BF16)
     core = lax.axis_index("c")
     home = pl.multiple_of(core * HALF, HALF)
     block = state[...]
@@ -234,33 +238,41 @@
     return out + jnp.dot(a_high, b_high, preferred_element_type=F32)
 
 
-def one_pass(state, residual, tables, paired):
+def one_pass(state, residual, weight, beside=None):
     sub = lax.broadcasted_iota(jnp.int32, (8, N), 0)
-    half = jnp.where(lanes_of(8) < K, 0, K)
     for k in range(K):
         t, s = divmod(k, 8)
-        for h, r, table in zip(state, residual, tables):
+        if beside is not None:
+            beside(k)
+        for i, (h, r) in enumerate(zip(state, residual)):
             change = jnp.maximum(-h[t], r[t])
             spread = jnp.broadcast_to(change[s : s + 1], (8, N))
             h[t] = jnp.where(sub == s, h[t] + change, h[t])
             for j in range(t if s < 7 else t + 1, K // 8):
-                weight = table[8 * j : 8 * j + 8]
-                if paired:
-                    weight = jnp.take_along_axis(weight, half + k, axis=1, mode="promise_in_bounds")
-                else:
-                    weight = jnp.broadcast_to(weight[:, k : k + 1], (8, N))
-                r[j] = r[j] - weight * spread
+                r[j] = r[j] - weight(i, k, j) * spread
     return [jnp.concatenate(h, axis=0) for h in state]
+
+
+def column_of(table, k, j):
+    return jnp.broadcast_to(table[8 * j : 8 * j + 8, k : k + 1], (8, N))
+
+
+def columns_of(table, k, j):
+    half = jnp.where(lanes_of(8) < K, k, K + k)
+    return jnp.take_along_axis(table[8 * j : 8 * j + 8], half, axis=1, mode="promise_in_bounds")
 
 
 def both_halves(x):
     return x + swapped(x)
 
 
-def shared_pass(shared, gram, carried):
-    inverse = 1.0 / jnp.maximum(diagonal(gram[:, :K]), 1.0)
+def shared_start(shared, gram, inverse, carried):
     start = carried - dot_split(gram, jnp.concatenate([shared, jnp.zeros((K, N), F32)], axis=0))
-    return one_pass([rows_of(shared)], [rows_of(start * inverse)], [gram * inverse], False)[0]
+    return [rows_of(shared)], [rows_of(start * inverse)]
+
+
+def shared_scale(gram):
+    return 1.0 / jnp.maximum(diagonal(gram[:, :K]), 1.0)
 
 
 def ridge_scale(gram):
@@ -270,7 +282,7 @@
     return 1.0 / jnp.maximum(RIDGE * jnp.where(lanes_of(K) < K, left, right), 1.0)
 
 
-def update_kernel(came, w_own, out, stats, grams_next, v_first):
+def update_kernel(came, w_own, spread, out, stats, grams_next, v_first, wide, later_shared, later_own):
     at_y, at_xl = lax.axis_index("y"), lax.axis_index("xl")
     pairs = range(4)
     stat, base, grams = [], [], []
@@ -282,34 +294,66 @@
         first, both = unfold_grams(came[a, K + K // 2 :], came[b, K + K // 2 :])
         grams.append(first)
         grams_next[p] = both
-    wide = w_own[...]
-    shared = jnp.where(at_xl == 0, left_left(wide, wide), right_right(wide, wide))
+    shared = w_own[...]
+    shared = jnp.where(at_xl == 0, left_left(shared, shared), right_right(shared, shared))
+
+    inverses = [ridge_scale(gram) for gram in grams]
+    parts = []
+    for p in pairs:
+        high, low = split((RIDGE * grams[p]) * inverses[p])
+        parts.append(jnp.concatenate([high.astype(F32), low.astype(F32)], axis=1))
+
+    def widen(k):
+        if k % 8:
+            return
+        rows = K - k
+        left = jnp.concatenate([part[k:] for part in parts], axis=0).astype(BF16)
+        columns = jnp.dot(left, spread[:, N * k : N * k + 8 * N], preferred_element_type=F32)
+        for i in range(8):
+            for p in pairs:
+                wide[k + i, K * p + k : K * p + K] = columns[rows * p : rows * p + rows, N * i : N * i + N]
 
     pulls = [dot_split(grams[p], corners(base[p])) for p in pairs]
     carried = sum(stat[p] - pulls[p] for p in pairs)
-    shared = shared_pass(shared, both_halves(sum(grams)), both_halves(carried))
+    total = both_halves(sum(grams))
+    scale = shared_scale(total)
+    table = total * scale
+    state, residual = shared_start(shared, total, scale, both_halves(carried))
+    (shared,) = one_pass(state, residual, lambda i, k, j: column_of(table, k, j), widen)
+
+    later = [grams_next[p] for p in pairs]
+    later_total = both_halves(sum(later))
+    later_scale = shared_scale(later_total)
+    later_table = later_total * later_scale
+    own = grams_next[at_y]
+    own_scale = ridge_scale(own)
+    own_table = (RIDGE * own) * own_scale
+
+    def prepare(k):
+        for j in range(k // 8, K // 8):
+            later_shared[k, 8 * j : 8 * j + 8] = column_of(later_table, k, j)
+            later_own[k, 8 * j : 8 * j + 8] = columns_of(own_table, k, j)
 
     pushed = dot_split(jnp.concatenate(grams, axis=0), corners(shared))
-    state, residual, tables = [], [], []
+    state, residual = [], []
     for p in pairs:
-        inverse = ridge_scale(grams[p])
         rest = stat[p] - pushed[K * p : K * p + K] - RIDGE * pulls[p]
         state.append(rows_of(base[p]))
-        residual.append(rows_of(rest * inverse))
-        tables.append((RIDGE * grams[p]) * inverse)
-    values = one_pass(state, residual, tables, True)
+        residual.append(rows_of(rest * inverses[p]))
+    values = one_pass(state, residual, lambda i, k, j: wide[k, K * i + 8 * j : K * i + 8 * j + 8], prepare)
     for p in pairs:
         v_first[p] = values[p]
 
-    later = [grams_next[p] for p in pairs]
     pulled = dot_split(jnp.concatenate(later, axis=1), jnp.concatenate([corners(v) for v in values], axis=0))
     carried = sum(stats[p] for p in pairs) - pulled
-    shared = shared_pass(shared, both_halves(sum(later)), both_halves(carried))
-
-    gram, specific = grams_next[at_y], v_first[at_y]
-    inverse = ridge_scale(gram)
-    rest = stats[at_y] - dot_split(gram, corners(shared + RIDGE * specific))
-    (specific,) = one_pass([rows_of(specific)], [rows_of(rest * inverse)], [(RIDGE * gram) * inverse], True)
+    state, residual = shared_start(shared, later_total, later_scale, both_halves(carried))
+    (shared,) = one_pass(state, residual, lambda i, k, j: later_shared[k, 8 * j : 8 * j + 8])
+
+    specific = v_first[at_y]
+    rest = stats[at_y] - dot_split(own, corners(shared + RIDGE * specific))
+    (specific,) = one_pass(
+        [rows_of(specific)], [rows_of(rest * own_scale)], lambda i, k, j: later_own[k, 8 * j : 8 * j + 8]
+    )
     pieces = (left_left(shared, specific), jnp.where(lanes_of(K) < K, shared, specific))
     for i in range(16):
         out[i] = pieces[i // 8]
@@ -382,13 +426,13 @@
         ],
     )(picks, dataset_id, sweep_count, expression, shared_init, specific_init)
     came = lax.ppermute(send, "c", SWAP)
-    keep, loads = pl.pallas_call(
+    keep, loads, spreader = pl.pallas_call(
         keep_kernel,
         name="keep",
         compiler_params=LIMIT,
-        out_shape=(near(HALF, N), shape(2, K, N)),
+        out_shape=(near(HALF, N), shape(2, K, N), pltpu.VMEM((2 * N, K * N), BF16)),
         in_specs=[VM, VM],
-        out_specs=[VM, VM],
+        out_specs=[VM] * 3,
     )(held(cells), held(state))
     packed = pl.pallas_call(
         pack_kernel,
@@ -408,10 +452,12 @@
         name="update",
         compiler_params=LIMIT,
         out_shape=near(16, K, N),
-        in_specs=[VM, VM],
+        in_specs=[VM] * 3,
         out_specs=VM,
-        scratch_shapes=[pltpu.VMEM((4, K, N), F32)] * 3,
-    )(held(came), held(w_own))
+        scratch_shapes=[pltpu.VMEM((4, K, N), F32)] * 3
+        + [pltpu.VMEM((K, 4 * K, N), F32)]
+        + [pltpu.VMEM((K, K, N), F32)] * 2,
+    )(held(came), held(w_own), held(spreader))
     mine = lax.all_to_all(spread, PLANE, 0, 0, tiled=True)
     other = lax.ppermute(mine, "c", SWAP)
     bases = finish(mine, lambda: lax.axis_index("c"), "mine")

time: 65.5 us -> 65.3 us (level)
  blocking collectives: 46.1 us -> 47.2 us
  waiting for transfers between devices: 1.34 us -> 0.56 us
    pallas_call x1, Pallas kernels: 0.78 us -> 1.69 us  [on_device(): pl.pallas_call(keep_kernel, name='keep', compiler_params=LIMIT, out_shape...]
    pallas_call x1, Pallas kernels: 4.03 us -> 3.13 us  [on_device(): pl.pallas_call(update_kernel, name='update', compiler_params=LIMIT, out_s...]
    ppermute x1, waiting for transfers between devices: 0.79 us -> 0.01 us  [on_device(): came = lax.ppermute(send, 'c', SWAP)]
    all_to_all x1, blocking collectives: 13.3 us -> 14.1 us  [on_device(): mine = lax.all_to_all(spread, PLANE, 0, 0, tiled=True)]
  transfers between devices with their start and end apart: 2 -> 2, of which waited for: 2 -> 1; matrix products, arithmetic and copies ran while one was open for 0% -> 0% of each run, Pallas kernels for 3% -> 4%
where the time goes in v6:
time: 65.3 us; the launch traced here: 65.2 us
  blocking collectives  47.2 us (72%)
  Pallas kernels  11.9 us (18%)
  starting transfers between devices  4.81 us (7%)
  between operations  0.66 us (1%)
    all_to_all x1, blocking collectives, on_device(): came = lax.all_to_all(packed, RING, 0, 0, tiled=True)  19.8 us
    all_to_all x1, blocking collectives, on_device(): mine = lax.all_to_all(spread, PLANE, 0, 0, tiled=True)  14.1 us
    all_to_all x1, blocking collectives, on_device(): came = lax.all_to_all(spread, GRP, 0, 0, tiled=True)  13.3 us
    pallas_call x1, Pallas kernels, on_device(): pl.pallas_call(front_kernel, name='front', out_shape=(near(HALF + PACKED,...  4.91 us
    ppermute x1, starting transfers between devices, on_device(): other = lax.ppermute(mine, 'c', SWAP)  3.35 us
    pallas_call x1, Pallas kernels, on_device(): pl.pallas_call(update_kernel, name='update', compiler_params=LIMIT, out_s...  3.13 us
    pallas_call x2, Pallas kernels, finish(): pl.pallas_call(finish_kernel, name=name, compiler_params=LIMIT, grid=(1,)...  1.96 us
    pallas_call x1, Pallas kernels, on_device(): pl.pallas_call(keep_kernel, name='keep', compiler_params=LIMIT, out_shape...  1.69 us
  transfers between devices with their start and end apart: 2, of which 1 were waited for; matrix products, arithmetic and copies ran while one was open for 0% of the time, Pallas kernels for 4%

profile of v6, /device:TPU:1, one launch (start us, length us, event | category | flops | bytes accessed | tf_op | source)
XLA Modules:
  0.0 65.2 jit_solution(17855907615076052214)
XLA Ops:
  0.6 4.9 %front.1 = (f32[1064,128]{1,0:T(8,128)S(1)}, bf16[2048,256]{1,0:T(8,128)(2,1)S(1)}, f32[128,256]{1,0:T(8,128)S(1)}, f32[64,128]{1,0:T(8,128)S(1)}, f32[64,128]{1,0:T(8,128)S(1)}) custom-call(s32[2,128]{1,0:T(2,128)} %picks_hbm.1, s32[512]{0:T(512)} %ids_hbm.1, s32[8]{0:T(128)} %sweeps_hbm.1, bf16[2000,512]{1,0:T(8,128)(2,1)} %x_hbm.1, f32[64,2000]{1,0:T(8,128)} %w_hbm.1, ...), custom_call_target="tpu_custom_call" | custom-call | tf_op jit(solution)/shard_map/front/pallas_call | solution.py:404
  5.6 1.5 %collective-permute-start = (f32[1064,128]{1,0:T(8,128)S(1)}, f32[1064,128]{1,0:T(8,128)S(1)}, u32[]{:S(2)}, u32[]{:S(2)}) collective-permute-start(f32[1064,128]{1,0:T(8,128)S(1)} %get-tuple-element.19.send), channel_id=1, source_target_pairs={{0,1},{1,0},{2,3},{3,2},{4,5},{5,4},{6,7},{7,6},{8,9},{9,8},{10,11... | collective-permute-start | bytes 1634312 | tf_op jit(solution)/shard_map/ppermute | solution.py:428
  7.0 1.7 %keep.1 = (f32[1024,128]{1,0:T(8,128)S(1)}, f32[2,64,128]{2,1,0:T(8,128)}, bf16[256,8192]{1,0:T(8,128)(2,1)S(1)}) custom-call(bf16[2048,256]{1,0:T(8,128)(2,1)S(1)} %get-tuple-element.15.cells, f32[128,256]{1,0:T(8,128)S(1)} %get-tuple-element.16.state), custom_call_target="tpu_custom_call" | custom-call | tf_op jit(solution)/shard_map/keep/pallas_call | solution.py:429
  8.7 0.0 collective-permute-done.came
  8.7 0.1 pack.1
  8.8 19.8 %all_to_all.15.came = f32[8,168,128]{2,1,0:T(8,128)S(1)} all-to-all(f32[8,168,128]{2,1,0:T(8,128)S(1)} %pack.1), channel_id=1, replica_groups=mesh['y'=4,'xl'=2,'xh'=2,'z'=4,'c'=2] {'xh','z'}, dimensions={0} | all-to-all | bytes 1376256 | tf_op jit(solution)/shard_map/all_to_all | solution.py:445
  28.6 0.2 group.1
  28.8 13.3 %all_to_all.16.came = f32[8,136,128]{2,1,0:T(8,128)S(1)} all-to-all(f32[8,136,128]{2,1,0:T(8,128)S(1)} %group.1), channel_id=1, replica_groups=mesh['y'=4,'xl'=2,'xh'=2,'z'=4,'c'=2] {'y','xl'}, dimensions={0} | all-to-all | bytes 1114112 | tf_op jit(solution)/shard_map/all_to_all | solution.py:449
  42.1 3.1 %update.1 = f32[16,64,128]{2,1,0:T(8,128)S(1)} custom-call(f32[8,136,128]{2,1,0:T(8,128)S(1)} %all_to_all.16.came, f32[64,128]{1,0:T(8,128)S(1)} %get-tuple-element.21.w_own, bf16[256,8192]{1,0:T(8,128)(2,1)S(1)} %get-tuple-element.22.spread), custom_call_target="tpu_custom_call" | custom-call | tf_op jit(solution)/shard_map/update/pallas_call | solution.py:450
  45.2 14.1 %all_to_all.17.part = f32[16,64,128]{2,1,0:T(8,128)S(1)} all-to-all(f32[16,64,128]{2,1,0:T(8,128)S(1)} %update.1), channel_id=1, replica_groups=mesh['y'=4,'xl'=2,'xh'=2,'z'=4,'c'=2] {'xl','xh','z'}, dimensions={0} | all-to-all | bytes 1048576 | tf_op jit(solution)/shard_map/all_to_all | solution.py:461
  59.3 3.3 %collective-permute-start.1 = (f32[16,64,128]{2,1,0:T(8,128)S(1)}, f32[16,64,128]{2,1,0:T(8,128)S(1)}, u32[]{:S(2)}, u32[]{:S(2)}) collective-permute-start(f32[16,64,128]{2,1,0:T(8,128)S(1)} %all_to_all.17.part), channel_id=1, source_target_pairs={{0,1},{1,0},{2,3},{3,2},{4,5},{5,4},{6,7},{7,6},{8,9},{9,8},{10,11... | collective-permute-start | bytes 1572872 | tf_op jit(solution)/shard_map/ppermute | solution.py:462
  62.7 1.0 %mine.1 = (f32[64,2000]{1,0:T(8,128)}, f32[1,64,2000]{2,1,0:T(8,128)}) custom-call(f32[16,64,128]{2,1,0:T(8,128)S(1)} %all_to_all.17.part), custom_call_target="tpu_custom_call" | custom-call | tf_op jit(solution)/shard_map/mine/pallas_call | solution.py:370
  63.7 0.6 collective-permute-done.1.part
  64.2 1.0 %other.1 = (f32[64,2000]{1,0:T(8,128)}, f32[1,64,2000]{2,1,0:T(8,128)}) custom-call(f32[16,64,128]{2,1,0:T(8,128)S(1)} %collective-permute-done.1.part, f32[64,2000]{1,0:T(8,128)} %get-tuple-element.23.refs_0_, f32[1,64,2000]{2,1,0:T(8,128)} %get-tuple-element.24.refs_1_), custom_call_target="tpu_custom_call", output_to_operand_aliasing={{0}: (1, {}), {1}: (2, {})} | custom-call | tf_op jit(solution)/shard_map/other/pallas_call | solution.py:370
Async XLA Ops:
  5.6 3.2 %collective-permute-start = (f32[1064,128]{1,0:T(8,128)S(1)}, f32[1064,128]{1,0:T(8,128)S(1)}, u32[]{:S(2)}, u32[]{:S(2)}) collective-permute-start(f32[1064,128]{1,0:T(8,128)S(1)} %get-tuple-element.19.send), channel_id=1, source_target_pairs={{0,1},{1,0},{2,3},{3,2},{4,5},{5,4},{6,7},{7,6},{8,9},{9,8},{10,11... | collective-permute-start | bytes 1634312 | tf_op jit(solution)/shard_map/ppermute | solution.py:428
  59.3 4.9 %collective-permute-start.1 = (f32[16,64,128]{2,1,0:T(8,128)S(1)}, f32[16,64,128]{2,1,0:T(8,128)S(1)}, u32[]{:S(2)}, u32[]{:S(2)}) collective-permute-start(f32[16,64,128]{2,1,0:T(8,128)S(1)} %all_to_all.17.part), channel_id=1, source_target_pairs={{0,1},{1,0},{2,3},{3,2},{4,5},{5,4},{6,7},{7,6},{8,9},{9,8},{10,11... | collective-permute-start | bytes 1572872 | tf_op jit(solution)/shard_map/ppermute | solution.py:462

commit v7 on v6

--- a/solution.py
+++ b/solution.py
@@ -15,9 +15,10 @@
 LAMBDA = 5.0
 RIDGE = 1.0 + LAMBDA
 HIGHEST = lax.Precision.HIGHEST
-GRP = ("y", "xl")
+SLOTS = ("y", "xl")
+GRP = ("xl", "y")
 RING = ("xh", "z")
-PLANE = ("xl", "xh", "z")
+PLANE = ("xh", "xl", "z")
 ALL = ("y", "xl", "xh", "z", "c")
 NT = (((1,), (1,)), ((), ()))
 F32 = jnp.float32
@@ -43,12 +44,18 @@
     sub = lax.broadcasted_iota(jnp.int32, (8, N), 0)
     for k in range(K):
         t, s = divmod(k, 8)
-        for half, (h, r) in enumerate(zip(state, residual)):
-            change = jnp.maximum(-h[t], r[t])
+        if s == 0:
+            floors = [-h[t] for h in state]
+            changes = [None] * len(state)
+        for half, r in enumerate(residual):
+            change = jnp.maximum(floors[half], r[t])
             spread = jnp.broadcast_to(change[s : s + 1], (8, N))
-            h[t] = jnp.where(sub == s, h[t] + change, h[t])
+            changes[half] = change if s == 0 else jnp.where(sub >= s, change, changes[half])
             for j in range((t if s < 7 else t + 1) if last else 0, K // 8):
                 r[j] = r[j] - column(half, k, j) * spread
+        if s == 7:
+            for h, change in zip(state, changes):
+                h[t] = h[t] + change
     return [jnp.concatenate(h, axis=0) for h in state]
 
 
@@ -223,8 +230,8 @@
     stats = (left_left(first, second), right_right(first, second))
     bases = split_rows(v_own[...])
     for i in range(8):
-        out[i, :K] = stats[i % 2]
-        out[i, K : K + K // 2] = bases[i % 2]
+        out[i, :K] = stats[i // 4]
+        out[i, K : K + K // 2] = bases[i // 4]
         out[i, K + K // 2 :] = total[N:]
 
 
@@ -244,12 +251,18 @@
         t, s = divmod(k, 8)
         if beside is not None:
             beside(k)
-        for i, (h, r) in enumerate(zip(state, residual)):
-            change = jnp.maximum(-h[t], r[t])
+        if s == 0:
+            floors = [-h[t] for h in state]
+            changes = [None] * len(state)
+        for i, r in enumerate(residual):
+            change = jnp.maximum(floors[i], r[t])
             spread = jnp.broadcast_to(change[s : s + 1], (8, N))
-            h[t] = jnp.where(sub == s, h[t] + change, h[t])
+            changes[i] = change if s == 0 else jnp.where(sub >= s, change, changes[i])
             for j in range(t if s < 7 else t + 1, K // 8):
                 r[j] = r[j] - weight(i, k, j) * spread
+        if s == 7:
+            for h, change in zip(state, changes):
+                h[t] = h[t] + change
     return [jnp.concatenate(h, axis=0) for h in state]
 
 
@@ -287,7 +300,7 @@
     pairs = range(4)
     stat, base, grams = [], [], []
     for p in pairs:
-        a, b = 2 * p, 2 * p + 1
+        a, b = p, 4 + p
         stat.append(left_left(came[a, :K], came[b, :K]))
         stats[p] = right_right(came[a, :K], came[b, :K])
         base.append(pair_rows(came[a, K : K + K // 2], came[b, K : K + K // 2]))
@@ -356,14 +369,16 @@
     )
     pieces = (left_left(shared, specific), jnp.where(lanes_of(K) < K, shared, specific))
     for i in range(16):
-        out[i] = pieces[i // 8]
+        out[i] = pieces[i // 4 % 2]
 
 
 def finish_kernel(part, *refs):
     w, v = refs[-2:]
     for i in range(8):
-        w[:, N * i : N * i + N] = left_left(part[i], part[8 + i])
-        v[0, :, N * i : N * i + N] = right_right(part[i], part[8 + i])
+        left = part[i // 4 * 8 + i % 4]
+        right = part[i // 4 * 8 + i % 4 + 4]
+        w[:, N * i : N * i + N] = left_left(left, right)
+        v[0, :, N * i : N * i + N] = right_right(left, right)
 
 
 def finish(part, half, name, earlier=()):
@@ -470,7 +485,7 @@
     return jax.shard_map(
         on_device,
         mesh=fine,
-        in_specs=(P(None, ALL), P(ALL), P(GRP), P(), P(None, ALL), P(), P(GRP, None, None)),
-        out_specs=(P(None, None, ALL), P(), P(GRP, None, None)),
+        in_specs=(P(None, ALL), P(ALL), P(SLOTS), P(), P(None, ALL), P(), P(SLOTS, None, None)),
+        out_specs=(P(None, None, ALL), P(), P(SLOTS, None, None)),
         check_vma=False,
     )

time: 65.3 us -> 65 us (level)
  no operation moved by 1% of the time
where the time goes in v7:
time: 65 us; the launch traced here: 64.9 us
  blocking collectives  46.9 us (72%)
  Pallas kernels  11.8 us (18%)
  starting transfers between devices  5.02 us (8%)
  between operations  0.66 us (1%)
    all_to_all x1, blocking collectives, on_device(): came = lax.all_to_all(packed, RING, 0, 0, tiled=True)  19.8 us
    all_to_all x1, blocking collectives, on_device(): mine = lax.all_to_all(spread, PLANE, 0, 0, tiled=True)  14.2 us
    all_to_all x1, blocking collectives, on_device(): came = lax.all_to_all(spread, GRP, 0, 0, tiled=True)  12.8 us
    pallas_call x1, Pallas kernels, on_device(): pl.pallas_call(front_kernel, name='front', out_shape=(near(HALF + PACKED,...  4.83 us
    ppermute x1, starting transfers between devices, on_device(): other = lax.ppermute(mine, 'c', SWAP)  3.56 us
    pallas_call x1, Pallas kernels, on_device(): pl.pallas_call(update_kernel, name='update', compiler_params=LIMIT, out_s...  3.07 us
    pallas_call x2, Pallas kernels, finish(): pl.pallas_call(finish_kernel, name=name, compiler_params=LIMIT, grid=(1,)...  1.96 us
    pallas_call x1, Pallas kernels, on_device(): pl.pallas_call(keep_kernel, name='keep', compiler_params=LIMIT, out_shape...  1.69 us
  transfers between devices with their start and end apart: 2, of which 1 were waited for; matrix products, arithmetic and copies ran while one was open for 0% of the time, Pallas kernels for 4%

profile of v7, /device:TPU:1, one launch (start us, length us, event | category | flops | bytes accessed | tf_op | source)
XLA Modules:
  0.0 64.9 jit_solution(591628436995041723)
XLA Ops:
  0.6 4.8 %front.1 = (f32[1064,128]{1,0:T(8,128)S(1)}, bf16[2048,256]{1,0:T(8,128)(2,1)S(1)}, f32[128,256]{1,0:T(8,128)S(1)}, f32[64,128]{1,0:T(8,128)S(1)}, f32[64,128]{1,0:T(8,128)S(1)}) custom-call(s32[2,128]{1,0:T(2,128)} %picks_hbm.1, s32[512]{0:T(512)} %ids_hbm.1, s32[8]{0:T(128)} %sweeps_hbm.1, bf16[2000,512]{1,0:T(8,128)(2,1)} %x_hbm.1, f32[64,2000]{1,0:T(8,128)} %w_hbm.1, ...), custom_call_target="tpu_custom_call" | custom-call | tf_op jit(solution)/shard_map/front/pallas_call | solution.py:419
  5.5 1.5 %collective-permute-start = (f32[1064,128]{1,0:T(8,128)S(1)}, f32[1064,128]{1,0:T(8,128)S(1)}, u32[]{:S(2)}, u32[]{:S(2)}) collective-permute-start(f32[1064,128]{1,0:T(8,128)S(1)} %get-tuple-element.19.send), channel_id=1, source_target_pairs={{0,1},{1,0},{2,3},{3,2},{4,5},{5,4},{6,7},{7,6},{8,9},{9,8},{10,11... | collective-permute-start | bytes 1634312 | tf_op jit(solution)/shard_map/ppermute | solution.py:443
  6.9 1.7 %keep.1 = (f32[1024,128]{1,0:T(8,128)S(1)}, f32[2,64,128]{2,1,0:T(8,128)}, bf16[256,8192]{1,0:T(8,128)(2,1)S(1)}) custom-call(bf16[2048,256]{1,0:T(8,128)(2,1)S(1)} %get-tuple-element.15.cells, f32[128,256]{1,0:T(8,128)S(1)} %get-tuple-element.16.state), custom_call_target="tpu_custom_call" | custom-call | tf_op jit(solution)/shard_map/keep/pallas_call | solution.py:444
  8.6 0.0 collective-permute-done.came
  8.6 0.1 pack.1
  8.7 19.8 %all_to_all.15.came = f32[8,168,128]{2,1,0:T(8,128)S(1)} all-to-all(f32[8,168,128]{2,1,0:T(8,128)S(1)} %pack.1), channel_id=1, replica_groups=mesh['y'=4,'xl'=2,'xh'=2,'z'=4,'c'=2] {'xh','z'}, dimensions={0} | all-to-all | bytes 1376256 | tf_op jit(solution)/shard_map/all_to_all | solution.py:460
  28.5 0.2 group.1
  28.7 12.8 %all_to_all.16.came = f32[8,136,128]{2,1,0:T(8,128)S(1)} all-to-all(f32[8,136,128]{2,1,0:T(8,128)S(1)} %group.1), channel_id=1, replica_groups=mesh['y'=4,'xl'=2,'xh'=2,'z'=4,'c'=2] {'xl','y'}, dimensions={0} | all-to-all | bytes 1114112 | tf_op jit(solution)/shard_map/all_to_all | solution.py:464
  41.6 3.1 %update.1 = f32[16,64,128]{2,1,0:T(8,128)S(1)} custom-call(f32[8,136,128]{2,1,0:T(8,128)S(1)} %all_to_all.16.came, f32[64,128]{1,0:T(8,128)S(1)} %get-tuple-element.21.w_own, bf16[256,8192]{1,0:T(8,128)(2,1)S(1)} %get-tuple-element.22.spread), custom_call_target="tpu_custom_call" | custom-call | tf_op jit(solution)/shard_map/update/pallas_call | solution.py:465
  44.6 14.2 %all_to_all.17.part = f32[16,64,128]{2,1,0:T(8,128)S(1)} all-to-all(f32[16,64,128]{2,1,0:T(8,128)S(1)} %update.1), channel_id=1, replica_groups=mesh['y'=4,'xl'=2,'xh'=2,'z'=4,'c'=2] {'xh','xl','z'}, dimensions={0} | all-to-all | bytes 1048576 | tf_op jit(solution)/shard_map/all_to_all | solution.py:476
  58.9 3.6 %collective-permute-start.1 = (f32[16,64,128]{2,1,0:T(8,128)S(1)}, f32[16,64,128]{2,1,0:T(8,128)S(1)}, u32[]{:S(2)}, u32[]{:S(2)}) collective-permute-start(f32[16,64,128]{2,1,0:T(8,128)S(1)} %all_to_all.17.part), channel_id=1, source_target_pairs={{0,1},{1,0},{2,3},{3,2},{4,5},{5,4},{6,7},{7,6},{8,9},{9,8},{10,11... | collective-permute-start | bytes 1572872 | tf_op jit(solution)/shard_map/ppermute | solution.py:477
  62.4 1.0 %mine.1 = (f32[64,2000]{1,0:T(8,128)}, f32[1,64,2000]{2,1,0:T(8,128)}) custom-call(f32[16,64,128]{2,1,0:T(8,128)S(1)} %all_to_all.17.part), custom_call_target="tpu_custom_call" | custom-call | tf_op jit(solution)/shard_map/mine/pallas_call | solution.py:385
  63.4 0.6 collective-permute-done.1.part
  64.0 1.0 %other.1 = (f32[64,2000]{1,0:T(8,128)}, f32[1,64,2000]{2,1,0:T(8,128)}) custom-call(f32[16,64,128]{2,1,0:T(8,128)S(1)} %collective-permute-done.1.part, f32[64,2000]{1,0:T(8,128)} %get-tuple-element.23.refs_0_, f32[1,64,2000]{2,1,0:T(8,128)} %get-tuple-element.24.refs_1_), custom_call_target="tpu_custom_call", output_to_operand_aliasing={{0}: (1, {}), {1}: (2, {})} | custom-call | tf_op jit(solution)/shard_map/other/pallas_call | solution.py:385
Async XLA Ops:
  5.5 3.2 %collective-permute-start = (f32[1064,128]{1,0:T(8,128)S(1)}, f32[1064,128]{1,0:T(8,128)S(1)}, u32[]{:S(2)}, u32[]{:S(2)}) collective-permute-start(f32[1064,128]{1,0:T(8,128)S(1)} %get-tuple-element.19.send), channel_id=1, source_target_pairs={{0,1},{1,0},{2,3},{3,2},{4,5},{5,4},{6,7},{7,6},{8,9},{9,8},{10,11... | collective-permute-start | bytes 1634312 | tf_op jit(solution)/shard_map/ppermute | solution.py:443
  58.9 5.1 %collective-permute-start.1 = (f32[16,64,128]{2,1,0:T(8,128)S(1)}, f32[16,64,128]{2,1,0:T(8,128)S(1)}, u32[]{:S(2)}, u32[]{:S(2)}) collective-permute-start(f32[16,64,128]{2,1,0:T(8,128)S(1)} %all_to_all.17.part), channel_id=1, source_target_pairs={{0,1},{1,0},{2,3},{3,2},{4,5},{5,4},{6,7},{7,6},{8,9},{9,8},{10,11... | collective-permute-start | bytes 1572872 | tf_op jit(solution)/shard_map/ppermute | solution.py:477

commit v8 on v7

--- a/solution.py
+++ b/solution.py
@@ -17,7 +17,7 @@
 HIGHEST = lax.Precision.HIGHEST
 SLOTS = ("y", "xl")
 GRP = ("xl", "y")
-RING = ("xh", "z")
+RING = ("z", "xh")
 PLANE = ("xh", "xl", "z")
 ALL = ("y", "xl", "xh", "z", "c")
 NT = (((1,), (1,)), ((), ()))
@@ -125,7 +125,7 @@
     picks, ids, sweeps, x, w, v, choose, table, sems,
 ):
     core = lax.axis_index("c")
-    tile = core * 8 + lax.axis_index("xh") * 4 + lax.axis_index("z")
+    tile = core * 8 + lax.axis_index("z") * 2 + lax.axis_index("xh")
     copies = [
         pltpu.make_async_copy(source, target, sems.at[i])
         for i, (source, target) in enumerate(
@@ -375,8 +375,8 @@
 def finish_kernel(part, *refs):
     w, v = refs[-2:]
     for i in range(8):
-        left = part[i // 4 * 8 + i % 4]
-        right = part[i // 4 * 8 + i % 4 + 4]
+        left = part[i % 2 * 8 + i // 2]
+        right = part[i % 2 * 8 + i // 2 + 4]
         w[:, N * i : N * i + N] = left_left(left, right)
         v[0, :, N * i : N * i + N] = right_right(left, right)
 

time: 65 us -> 64.6 us (level)
  blocking collectives: 46.9 us -> 44.6 us
  Pallas kernels: 11.8 us -> 12.6 us
    all_to_all x1, blocking collectives: 14.2 us -> 12 us  [on_device(): mine = lax.all_to_all(spread, PLANE, 0, 0, tiled=True)]
    pallas_call x1, Pallas kernels: 4.83 us -> 5.61 us  [on_device(): pl.pallas_call(front_kernel, name='front', out_shape=(near(HALF + PACKED,...]
where the time goes in v8:
time: 64.6 us; the launch traced here: 63.9 us
  blocking collectives  44.6 us (69%)
  Pallas kernels  12.6 us (20%)
  starting transfers between devices  5.5 us (9%)
  between operations  0.66 us (1%)
    all_to_all x1, blocking collectives, on_device(): came = lax.all_to_all(packed, RING, 0, 0, tiled=True)  20.3 us
    all_to_all x1, blocking collectives, on_device(): came = lax.all_to_all(spread, GRP, 0, 0, tiled=True)  12.3 us
    all_to_all x1, blocking collectives, on_device(): mine = lax.all_to_all(spread, PLANE, 0, 0, tiled=True)  12 us
    pallas_call x1, Pallas kernels, on_device(): pl.pallas_call(front_kernel, name='front', out_shape=(near(HALF + PACKED,...  5.61 us
    ppermute x1, starting transfers between devices, on_device(): other = lax.ppermute(mine, 'c', SWAP)  4.03 us
    pallas_call x1, Pallas kernels, on_device(): pl.pallas_call(update_kernel, name='update', compiler_params=LIMIT, out_s...  3.07 us
    pallas_call x2, Pallas kernels, finish(): pl.pallas_call(finish_kernel, name=name, compiler_params=LIMIT, grid=(1,)...  1.96 us
    pallas_call x1, Pallas kernels, on_device(): pl.pallas_call(keep_kernel, name='keep', compiler_params=LIMIT, out_shape...  1.69 us
  transfers between devices with their start and end apart: 2, of which 1 were waited for; matrix products, arithmetic and copies ran while one was open for 0% of the time, Pallas kernels for 4%

profile of v8, /device:TPU:1, one launch (start us, length us, event | category | flops | bytes accessed | tf_op | source)
XLA Modules:
  0.0 63.9 jit_solution(13104592567795320903)
XLA Ops:
  0.6 5.6 %front.1 = (f32[1064,128]{1,0:T(8,128)S(1)}, bf16[2048,256]{1,0:T(8,128)(2,1)S(1)}, f32[128,256]{1,0:T(8,128)S(1)}, f32[64,128]{1,0:T(8,128)S(1)}, f32[64,128]{1,0:T(8,128)S(1)}) custom-call(s32[2,128]{1,0:T(2,128)} %picks_hbm.1, s32[512]{0:T(512)} %ids_hbm.1, s32[8]{0:T(128)} %sweeps_hbm.1, bf16[2000,512]{1,0:T(8,128)(2,1)} %x_hbm.1, f32[64,2000]{1,0:T(8,128)} %w_hbm.1, ...), custom_call_target="tpu_custom_call" | custom-call | tf_op jit(solution)/shard_map/front/pallas_call | solution.py:419
  6.3 1.5 %collective-permute-start = (f32[1064,128]{1,0:T(8,128)S(1)}, f32[1064,128]{1,0:T(8,128)S(1)}, u32[]{:S(2)}, u32[]{:S(2)}) collective-permute-start(f32[1064,128]{1,0:T(8,128)S(1)} %get-tuple-element.19.send), channel_id=1, source_target_pairs={{0,1},{1,0},{2,3},{3,2},{4,5},{5,4},{6,7},{7,6},{8,9},{9,8},{10,11... | collective-permute-start | bytes 1634312 | tf_op jit(solution)/shard_map/ppermute | solution.py:443
  7.7 1.7 %keep.1 = (f32[1024,128]{1,0:T(8,128)S(1)}, f32[2,64,128]{2,1,0:T(8,128)}, bf16[256,8192]{1,0:T(8,128)(2,1)S(1)}) custom-call(bf16[2048,256]{1,0:T(8,128)(2,1)S(1)} %get-tuple-element.15.cells, f32[128,256]{1,0:T(8,128)S(1)} %get-tuple-element.16.state), custom_call_target="tpu_custom_call" | custom-call | tf_op jit(solution)/shard_map/keep/pallas_call | solution.py:444
  9.4 0.0 collective-permute-done.came
  9.4 0.1 pack.1
  9.5 20.3 %all_to_all.15.came = f32[8,168,128]{2,1,0:T(8,128)S(1)} all-to-all(f32[8,168,128]{2,1,0:T(8,128)S(1)} %pack.1), channel_id=1, replica_groups=mesh['y'=4,'xl'=2,'xh'=2,'z'=4,'c'=2] {'z','xh'}, dimensions={0} | all-to-all | bytes 1376256 | tf_op jit(solution)/shard_map/all_to_all | solution.py:460
  29.8 0.2 group.1
  30.0 12.3 %all_to_all.16.came = f32[8,136,128]{2,1,0:T(8,128)S(1)} all-to-all(f32[8,136,128]{2,1,0:T(8,128)S(1)} %group.1), channel_id=1, replica_groups=mesh['y'=4,'xl'=2,'xh'=2,'z'=4,'c'=2] {'xl','y'}, dimensions={0} | all-to-all | bytes 1114112 | tf_op jit(solution)/shard_map/all_to_all | solution.py:464
  42.3 3.1 %update.1 = f32[16,64,128]{2,1,0:T(8,128)S(1)} custom-call(f32[8,136,128]{2,1,0:T(8,128)S(1)} %all_to_all.16.came, f32[64,128]{1,0:T(8,128)S(1)} %get-tuple-element.21.w_own, bf16[256,8192]{1,0:T(8,128)(2,1)S(1)} %get-tuple-element.22.spread), custom_call_target="tpu_custom_call" | custom-call | tf_op jit(solution)/shard_map/update/pallas_call | solution.py:465
  45.4 12.0 %all_to_all.17.part = f32[16,64,128]{2,1,0:T(8,128)S(1)} all-to-all(f32[16,64,128]{2,1,0:T(8,128)S(1)} %update.1), channel_id=1, replica_groups=mesh['y'=4,'xl'=2,'xh'=2,'z'=4,'c'=2] {'xh','xl','z'}, dimensions={0} | all-to-all | bytes 1048576 | tf_op jit(solution)/shard_map/all_to_all | solution.py:476
  57.4 4.0 %collective-permute-start.1 = (f32[16,64,128]{2,1,0:T(8,128)S(1)}, f32[16,64,128]{2,1,0:T(8,128)S(1)}, u32[]{:S(2)}, u32[]{:S(2)}) collective-permute-start(f32[16,64,128]{2,1,0:T(8,128)S(1)} %all_to_all.17.part), channel_id=1, source_target_pairs={{0,1},{1,0},{2,3},{3,2},{4,5},{5,4},{6,7},{7,6},{8,9},{9,8},{10,11... | collective-permute-start | bytes 1572872 | tf_op jit(solution)/shard_map/ppermute | solution.py:477
  61.4 1.0 %mine.1 = (f32[64,2000]{1,0:T(8,128)}, f32[1,64,2000]{2,1,0:T(8,128)}) custom-call(f32[16,64,128]{2,1,0:T(8,128)S(1)} %all_to_all.17.part), custom_call_target="tpu_custom_call" | custom-call | tf_op jit(solution)/shard_map/mine/pallas_call | solution.py:385
  62.4 0.6 collective-permute-done.1.part
  63.0 1.0 %other.1 = (f32[64,2000]{1,0:T(8,128)}, f32[1,64,2000]{2,1,0:T(8,128)}) custom-call(f32[16,64,128]{2,1,0:T(8,128)S(1)} %collective-permute-done.1.part, f32[64,2000]{1,0:T(8,128)} %get-tuple-element.23.refs_0_, f32[1,64,2000]{2,1,0:T(8,128)} %get-tuple-element.24.refs_1_), custom_call_target="tpu_custom_call", output_to_operand_aliasing={{0}: (1, {}), {1}: (2, {})} | custom-call | tf_op jit(solution)/shard_map/other/pallas_call | solution.py:385
Async XLA Ops:
  6.3 3.2 %collective-permute-start = (f32[1064,128]{1,0:T(8,128)S(1)}, f32[1064,128]{1,0:T(8,128)S(1)}, u32[]{:S(2)}, u32[]{:S(2)}) collective-permute-start(f32[1064,128]{1,0:T(8,128)S(1)} %get-tuple-element.19.send), channel_id=1, source_target_pairs={{0,1},{1,0},{2,3},{3,2},{4,5},{5,4},{6,7},{7,6},{8,9},{9,8},{10,11... | collective-permute-start | bytes 1634312 | tf_op jit(solution)/shard_map/ppermute | solution.py:443
  57.4 5.6 %collective-permute-start.1 = (f32[16,64,128]{2,1,0:T(8,128)S(1)}, f32[16,64,128]{2,1,0:T(8,128)S(1)}, u32[]{:S(2)}, u32[]{:S(2)}) collective-permute-start(f32[16,64,128]{2,1,0:T(8,128)S(1)} %all_to_all.17.part), channel_id=1, source_target_pairs={{0,1},{1,0},{2,3},{3,2},{4,5},{5,4},{6,7},{7,6},{8,9},{9,8},{10,11... | collective-permute-start | bytes 1572872 | tf_op jit(solution)/shard_map/ppermute | solution.py:477

commit v9 on v8

--- a/solution.py
+++ b/solution.py
@@ -197,8 +197,12 @@
     )
     state[...] = block
     away = pl.multiple_of((1 - core) * HALF, HALF)
-    send[:HALF] = dot_nt(cells[pl.ds(away, HALF)], block.astype(BF16))
-    send[HALF:] = fold_grams(dot_nt(both, block, HIGHEST))
+    high, low = split(both)
+    rounded = block.astype(BF16)
+    gram = dot_nt(jnp.concatenate([high, low], axis=0), rounded)
+    gram = gram[:K] + gram[K:] + dot_nt(high, split(block)[1])
+    send[HALF:] = fold_grams(gram)
+    send[:HALF] = dot_nt(cells[pl.ds(away, HALF)], rounded)
 
 
 def keep_kernel(cells, state, keep, loads, spread):

time: 64.6 us -> 64.2 us (level)
  Pallas kernels: 12.6 us -> 11.4 us
  blocking collectives: 44.6 us -> 45.4 us
    pallas_call x1, Pallas kernels: 5.61 us -> 4.46 us  [on_device(): pl.pallas_call(front_kernel, name='front', out_shape=(near(HALF + PACKED,...]
where the time goes in v9:
time: 64.2 us; the launch traced here: 63.6 us
  blocking collectives  45.4 us (71%)
  Pallas kernels  11.4 us (18%)
  starting transfers between devices  5.49 us (9%)
  between operations  0.66 us (1%)
    all_to_all x1, blocking collectives, on_device(): came = lax.all_to_all(packed, RING, 0, 0, tiled=True)  20.3 us
    all_to_all x1, blocking collectives, on_device(): came = lax.all_to_all(spread, GRP, 0, 0, tiled=True)  12.9 us
    all_to_all x1, blocking collectives, on_device(): mine = lax.all_to_all(spread, PLANE, 0, 0, tiled=True)  12.2 us
    pallas_call x1, Pallas kernels, on_device(): pl.pallas_call(front_kernel, name='front', out_shape=(near(HALF + PACKED,...  4.46 us
    ppermute x1, starting transfers between devices, on_device(): other = lax.ppermute(mine, 'c', SWAP)  4.03 us
    pallas_call x1, Pallas kernels, on_device(): pl.pallas_call(update_kernel, name='update', compiler_params=LIMIT, out_s...  3.07 us
    pallas_call x2, Pallas kernels, finish(): pl.pallas_call(finish_kernel, name=name, compiler_params=LIMIT, grid=(1,)...  1.96 us
    pallas_call x1, Pallas kernels, on_device(): pl.pallas_call(keep_kernel, name='keep', compiler_params=LIMIT, out_shape...  1.69 us
  transfers between devices with their start and end apart: 2, of which 1 were waited for; matrix products, arithmetic and copies ran while one was open for 0% of the time, Pallas kernels for 4%

profile of v9, /device:TPU:1, one launch (start us, length us, event | category | flops | bytes accessed | tf_op | source)
XLA Modules:
  0.0 63.6 jit_solution(3264611131740902901)
XLA Ops:
  0.6 4.5 %front.1 = (f32[1064,128]{1,0:T(8,128)S(1)}, bf16[2048,256]{1,0:T(8,128)(2,1)S(1)}, f32[128,256]{1,0:T(8,128)S(1)}, f32[64,128]{1,0:T(8,128)S(1)}, f32[64,128]{1,0:T(8,128)S(1)}) custom-call(s32[2,128]{1,0:T(2,128)} %picks_hbm.1, s32[512]{0:T(512)} %ids_hbm.1, s32[8]{0:T(128)} %sweeps_hbm.1, bf16[2000,512]{1,0:T(8,128)(2,1)} %x_hbm.1, f32[64,2000]{1,0:T(8,128)} %w_hbm.1, ...), custom_call_target="tpu_custom_call" | custom-call | tf_op jit(solution)/shard_map/front/pallas_call | solution.py:423
  5.1 1.5 %collective-permute-start = (f32[1064,128]{1,0:T(8,128)S(1)}, f32[1064,128]{1,0:T(8,128)S(1)}, u32[]{:S(2)}, u32[]{:S(2)}) collective-permute-start(f32[1064,128]{1,0:T(8,128)S(1)} %get-tuple-element.19.send), channel_id=1, source_target_pairs={{0,1},{1,0},{2,3},{3,2},{4,5},{5,4},{6,7},{7,6},{8,9},{9,8},{10,11... | collective-permute-start | bytes 1634312 | tf_op jit(solution)/shard_map/ppermute | solution.py:447
  6.6 1.7 %keep.1 = (f32[1024,128]{1,0:T(8,128)S(1)}, f32[2,64,128]{2,1,0:T(8,128)}, bf16[256,8192]{1,0:T(8,128)(2,1)S(1)}) custom-call(bf16[2048,256]{1,0:T(8,128)(2,1)S(1)} %get-tuple-element.15.cells, f32[128,256]{1,0:T(8,128)S(1)} %get-tuple-element.16.state), custom_call_target="tpu_custom_call" | custom-call | tf_op jit(solution)/shard_map/keep/pallas_call | solution.py:448
  8.3 0.0 collective-permute-done.came
  8.3 0.1 pack.1
  8.3 20.3 %all_to_all.15.came = f32[8,168,128]{2,1,0:T(8,128)S(1)} all-to-all(f32[8,168,128]{2,1,0:T(8,128)S(1)} %pack.1), channel_id=1, replica_groups=mesh['y'=4,'xl'=2,'xh'=2,'z'=4,'c'=2] {'z','xh'}, dimensions={0} | all-to-all | bytes 1376256 | tf_op jit(solution)/shard_map/all_to_all | solution.py:464
  28.6 0.2 group.1
  28.8 12.9 %all_to_all.16.came = f32[8,136,128]{2,1,0:T(8,128)S(1)} all-to-all(f32[8,136,128]{2,1,0:T(8,128)S(1)} %group.1), channel_id=1, replica_groups=mesh['y'=4,'xl'=2,'xh'=2,'z'=4,'c'=2] {'xl','y'}, dimensions={0} | all-to-all | bytes 1114112 | tf_op jit(solution)/shard_map/all_to_all | solution.py:468
  41.8 3.1 %update.1 = f32[16,64,128]{2,1,0:T(8,128)S(1)} custom-call(f32[8,136,128]{2,1,0:T(8,128)S(1)} %all_to_all.16.came, f32[64,128]{1,0:T(8,128)S(1)} %get-tuple-element.21.w_own, bf16[256,8192]{1,0:T(8,128)(2,1)S(1)} %get-tuple-element.22.spread), custom_call_target="tpu_custom_call" | custom-call | tf_op jit(solution)/shard_map/update/pallas_call | solution.py:469
  44.8 12.2 %all_to_all.17.part = f32[16,64,128]{2,1,0:T(8,128)S(1)} all-to-all(f32[16,64,128]{2,1,0:T(8,128)S(1)} %update.1), channel_id=1, replica_groups=mesh['y'=4,'xl'=2,'xh'=2,'z'=4,'c'=2] {'xh','xl','z'}, dimensions={0} | all-to-all | bytes 1048576 | tf_op jit(solution)/shard_map/all_to_all | solution.py:480
  57.0 4.0 %collective-permute-start.1 = (f32[16,64,128]{2,1,0:T(8,128)S(1)}, f32[16,64,128]{2,1,0:T(8,128)S(1)}, u32[]{:S(2)}, u32[]{:S(2)}) collective-permute-start(f32[16,64,128]{2,1,0:T(8,128)S(1)} %all_to_all.17.part), channel_id=1, source_target_pairs={{0,1},{1,0},{2,3},{3,2},{4,5},{5,4},{6,7},{7,6},{8,9},{9,8},{10,11... | collective-permute-start | bytes 1572872 | tf_op jit(solution)/shard_map/ppermute | solution.py:481
  61.1 1.0 %mine.1 = (f32[64,2000]{1,0:T(8,128)}, f32[1,64,2000]{2,1,0:T(8,128)}) custom-call(f32[16,64,128]{2,1,0:T(8,128)S(1)} %all_to_all.17.part), custom_call_target="tpu_custom_call" | custom-call | tf_op jit(solution)/shard_map/mine/pallas_call | solution.py:389
  62.0 0.6 collective-permute-done.1.part
  62.6 1.0 %other.1 = (f32[64,2000]{1,0:T(8,128)}, f32[1,64,2000]{2,1,0:T(8,128)}) custom-call(f32[16,64,128]{2,1,0:T(8,128)S(1)} %collective-permute-done.1.part, f32[64,2000]{1,0:T(8,128)} %get-tuple-element.23.refs_0_, f32[1,64,2000]{2,1,0:T(8,128)} %get-tuple-element.24.refs_1_), custom_call_target="tpu_custom_call", output_to_operand_aliasing={{0}: (1, {}), {1}: (2, {})} | custom-call | tf_op jit(solution)/shard_map/other/pallas_call | solution.py:389
Async XLA Ops:
  5.1 3.2 %collective-permute-start = (f32[1064,128]{1,0:T(8,128)S(1)}, f32[1064,128]{1,0:T(8,128)S(1)}, u32[]{:S(2)}, u32[]{:S(2)}) collective-permute-start(f32[1064,128]{1,0:T(8,128)S(1)} %get-tuple-element.19.send), channel_id=1, source_target_pairs={{0,1},{1,0},{2,3},{3,2},{4,5},{5,4},{6,7},{7,6},{8,9},{9,8},{10,11... | collective-permute-start | bytes 1634312 | tf_op jit(solution)/shard_map/ppermute | solution.py:447
  57.0 5.6 %collective-permute-start.1 = (f32[16,64,128]{2,1,0:T(8,128)S(1)}, f32[16,64,128]{2,1,0:T(8,128)S(1)}, u32[]{:S(2)}, u32[]{:S(2)}) collective-permute-start(f32[16,64,128]{2,1,0:T(8,128)S(1)} %all_to_all.17.part), channel_id=1, source_target_pairs={{0,1},{1,0},{2,3},{3,2},{4,5},{5,4},{6,7},{7,6},{8,9},{9,8},{10,11... | collective-permute-start | bytes 1572872 | tf_op jit(solution)/shard_map/ppermute | solution.py:481

commit v10 on v9

--- a/solution.py
+++ b/solution.py
@@ -240,13 +240,10 @@
 
 
 def dot_split(a, b):
-    a_high = a.astype(BF16)
-    b_high = b.astype(BF16)
-    a_low = (a - a_high.astype(F32)).astype(BF16)
-    b_low = (b - b_high.astype(F32)).astype(BF16)
-    out = jnp.dot(a_high, b_low, preferred_element_type=F32)
-    out = out + jnp.dot(a_low, b_high, preferred_element_type=F32)
-    return out + jnp.dot(a_high, b_high, preferred_element_type=F32)
+    a_high, a_low = split(a)
+    b_high, b_low = split(b)
+    left = jnp.concatenate([a_high, a_low, a_high], axis=1)
+    return jnp.dot(left, jnp.concatenate([b_high, b_high, b_low], axis=0), preferred_element_type=F32)
 
 
 def one_pass(state, residual, weight, beside=None):

time: 64.2 us -> 64.6 us (level)
  no operation moved by 1% of the time
where the time goes in v10:
time: 64.6 us; the launch traced here: 64.2 us
  blocking collectives  45.6 us (71%)
  Pallas kernels  11.9 us (18%)
  starting transfers between devices  5.49 us (8%)
  between operations  0.66 us (1%)
    all_to_all x1, blocking collectives, on_device(): came = lax.all_to_all(packed, RING, 0, 0, tiled=True)  20.3 us
    all_to_all x1, blocking collectives, on_device(): came = lax.all_to_all(spread, GRP, 0, 0, tiled=True)  13.3 us
    all_to_all x1, blocking collectives, on_device(): mine = lax.all_to_all(spread, PLANE, 0, 0, tiled=True)  12.1 us
    pallas_call x1, Pallas kernels, on_device(): pl.pallas_call(front_kernel, name='front', out_shape=(near(HALF + PACKED,...  4.86 us
    ppermute x1, starting transfers between devices, on_device(): other = lax.ppermute(mine, 'c', SWAP)  4.03 us
    pallas_call x1, Pallas kernels, on_device(): pl.pallas_call(update_kernel, name='update', compiler_params=LIMIT, out_s...  3.1 us
    pallas_call x2, Pallas kernels, finish(): pl.pallas_call(finish_kernel, name=name, compiler_params=LIMIT, grid=(1,)...  1.96 us
    pallas_call x1, Pallas kernels, on_device(): pl.pallas_call(keep_kernel, name='keep', compiler_params=LIMIT, out_shape...  1.69 us
  transfers between devices with their start and end apart: 2, of which 1 were waited for; matrix products, arithmetic and copies ran while one was open for 0% of the time, Pallas kernels for 4%

profile of v10, /device:TPU:1, one launch (start us, length us, event | category | flops | bytes accessed | tf_op | source)
XLA Modules:
  0.0 64.2 jit_solution(12622339946441438089)
XLA Ops:
  0.6 4.9 %front.1 = (f32[1064,128]{1,0:T(8,128)S(1)}, bf16[2048,256]{1,0:T(8,128)(2,1)S(1)}, f32[128,256]{1,0:T(8,128)S(1)}, f32[64,128]{1,0:T(8,128)S(1)}, f32[64,128]{1,0:T(8,128)S(1)}) custom-call(s32[2,128]{1,0:T(2,128)} %picks_hbm.1, s32[512]{0:T(512)} %ids_hbm.1, s32[8]{0:T(128)} %sweeps_hbm.1, bf16[2000,512]{1,0:T(8,128)(2,1)} %x_hbm.1, f32[64,2000]{1,0:T(8,128)} %w_hbm.1, ...), custom_call_target="tpu_custom_call" | custom-call | tf_op jit(solution)/shard_map/front/pallas_call | solution.py:420
  5.5 1.5 %collective-permute-start = (f32[1064,128]{1,0:T(8,128)S(1)}, f32[1064,128]{1,0:T(8,128)S(1)}, u32[]{:S(2)}, u32[]{:S(2)}) collective-permute-start(f32[1064,128]{1,0:T(8,128)S(1)} %get-tuple-element.19.send), channel_id=1, source_target_pairs={{0,1},{1,0},{2,3},{3,2},{4,5},{5,4},{6,7},{7,6},{8,9},{9,8},{10,11... | collective-permute-start | bytes 1634312 | tf_op jit(solution)/shard_map/ppermute | solution.py:444
  7.0 1.7 %keep.1 = (f32[1024,128]{1,0:T(8,128)S(1)}, f32[2,64,128]{2,1,0:T(8,128)}, bf16[256,8192]{1,0:T(8,128)(2,1)S(1)}) custom-call(bf16[2048,256]{1,0:T(8,128)(2,1)S(1)} %get-tuple-element.15.cells, f32[128,256]{1,0:T(8,128)S(1)} %get-tuple-element.16.state), custom_call_target="tpu_custom_call" | custom-call | tf_op jit(solution)/shard_map/keep/pallas_call | solution.py:445
  8.7 0.0 collective-permute-done.came
  8.7 0.1 pack.1
  8.7 20.3 %all_to_all.15.came = f32[8,168,128]{2,1,0:T(8,128)S(1)} all-to-all(f32[8,168,128]{2,1,0:T(8,128)S(1)} %pack.1), channel_id=1, replica_groups=mesh['y'=4,'xl'=2,'xh'=2,'z'=4,'c'=2] {'z','xh'}, dimensions={0} | all-to-all | bytes 1376256 | tf_op jit(solution)/shard_map/all_to_all | solution.py:461
  29.1 0.2 group.1
  29.2 13.3 %all_to_all.16.came = f32[8,136,128]{2,1,0:T(8,128)S(1)} all-to-all(f32[8,136,128]{2,1,0:T(8,128)S(1)} %group.1), channel_id=1, replica_groups=mesh['y'=4,'xl'=2,'xh'=2,'z'=4,'c'=2] {'xl','y'}, dimensions={0} | all-to-all | bytes 1114112 | tf_op jit(solution)/shard_map/all_to_all | solution.py:465
  42.5 3.1 %update.1 = f32[16,64,128]{2,1,0:T(8,128)S(1)} custom-call(f32[8,136,128]{2,1,0:T(8,128)S(1)} %all_to_all.16.came, f32[64,128]{1,0:T(8,128)S(1)} %get-tuple-element.21.w_own, bf16[256,8192]{1,0:T(8,128)(2,1)S(1)} %get-tuple-element.22.spread), custom_call_target="tpu_custom_call" | custom-call | tf_op jit(solution)/shard_map/update/pallas_call | solution.py:466
  45.6 12.1 %all_to_all.17.part = f32[16,64,128]{2,1,0:T(8,128)S(1)} all-to-all(f32[16,64,128]{2,1,0:T(8,128)S(1)} %update.1), channel_id=1, replica_groups=mesh['y'=4,'xl'=2,'xh'=2,'z'=4,'c'=2] {'xh','xl','z'}, dimensions={0} | all-to-all | bytes 1048576 | tf_op jit(solution)/shard_map/all_to_all | solution.py:477
  57.7 4.0 %collective-permute-start.1 = (f32[16,64,128]{2,1,0:T(8,128)S(1)}, f32[16,64,128]{2,1,0:T(8,128)S(1)}, u32[]{:S(2)}, u32[]{:S(2)}) collective-permute-start(f32[16,64,128]{2,1,0:T(8,128)S(1)} %all_to_all.17.part), channel_id=1, source_target_pairs={{0,1},{1,0},{2,3},{3,2},{4,5},{5,4},{6,7},{7,6},{8,9},{9,8},{10,11... | collective-permute-start | bytes 1572872 | tf_op jit(solution)/shard_map/ppermute | solution.py:478
  61.7 1.0 %mine.1 = (f32[64,2000]{1,0:T(8,128)}, f32[1,64,2000]{2,1,0:T(8,128)}) custom-call(f32[16,64,128]{2,1,0:T(8,128)S(1)} %all_to_all.17.part), custom_call_target="tpu_custom_call" | custom-call | tf_op jit(solution)/shard_map/mine/pallas_call | solution.py:386
  62.7 0.6 collective-permute-done.1.part
  63.2 1.0 %other.1 = (f32[64,2000]{1,0:T(8,128)}, f32[1,64,2000]{2,1,0:T(8,128)}) custom-call(f32[16,64,128]{2,1,0:T(8,128)S(1)} %collective-permute-done.1.part, f32[64,2000]{1,0:T(8,128)} %get-tuple-element.23.refs_0_, f32[1,64,2000]{2,1,0:T(8,128)} %get-tuple-element.24.refs_1_), custom_call_target="tpu_custom_call", output_to_operand_aliasing={{0}: (1, {}), {1}: (2, {})} | custom-call | tf_op jit(solution)/shard_map/other/pallas_call | solution.py:386
Async XLA Ops:
  5.5 3.2 %collective-permute-start = (f32[1064,128]{1,0:T(8,128)S(1)}, f32[1064,128]{1,0:T(8,128)S(1)}, u32[]{:S(2)}, u32[]{:S(2)}) collective-permute-start(f32[1064,128]{1,0:T(8,128)S(1)} %get-tuple-element.19.send), channel_id=1, source_target_pairs={{0,1},{1,0},{2,3},{3,2},{4,5},{5,4},{6,7},{7,6},{8,9},{9,8},{10,11... | collective-permute-start | bytes 1634312 | tf_op jit(solution)/shard_map/ppermute | solution.py:444
  57.7 5.6 %collective-permute-start.1 = (f32[16,64,128]{2,1,0:T(8,128)S(1)}, f32[16,64,128]{2,1,0:T(8,128)S(1)}, u32[]{:S(2)}, u32[]{:S(2)}) collective-permute-start(f32[16,64,128]{2,1,0:T(8,128)S(1)} %all_to_all.17.part), channel_id=1, source_target_pairs={{0,1},{1,0},{2,3},{3,2},{4,5},{5,4},{6,7},{7,6},{8,9},{9,8},{10,11... | collective-permute-start | bytes 1572872 | tf_op jit(solution)/shard_map/ppermute | solution.py:478

commit v11 on v10

--- a/solution.py
+++ b/solution.py
@@ -112,11 +112,6 @@
 def split(x):
     high = x.astype(BF16)
     return high, (x - high.astype(F32)).astype(BF16)
-
-
-def gram_of(high, low):
-    both = dot_nt(jnp.concatenate([high, low], axis=0), high)
-    return both[:K], both[K:]
 
 
 def front_kernel(
@@ -164,10 +159,11 @@
 
     specific = v[...]
     mixed_high, mixed_low = split(w[...] + specific)
-    mixed_gram, mixed_cross = gram_of(mixed_high, mixed_low)
-    own_gram, own_cross = gram_of(*split(specific))
-    cross = mixed_cross + LAMBDA * own_cross
-    gram = mixed_gram + LAMBDA * own_gram + cross + cross.T
+    own_high, own_low = split(specific)
+    both = dot_nt(jnp.concatenate([mixed_high, mixed_low], axis=0), mixed_high)
+    other = dot_nt(jnp.concatenate([own_high, own_low], axis=0), own_high)
+    total = both + LAMBDA * other
+    gram = total[:K] + total[K:] + total[K:].T
     inverse = 1.0 / (diagonal(gram) + EPSILON)
     scaled = gram * inverse
     for copy in copies[3:]:

time: 64.6 us -> 64.1 us (level)
  no operation moved by 1% of the time
where the time goes in v11:
time: 64.1 us; the launch traced here: 63.7 us
  blocking collectives  45.7 us (71%)
  Pallas kernels  11.3 us (18%)
  starting transfers between devices  5.49 us (9%)
  between operations  0.66 us (1%)
    all_to_all x1, blocking collectives, on_device(): came = lax.all_to_all(packed, RING, 0, 0, tiled=True)  20.3 us
    all_to_all x1, blocking collectives, on_device(): came = lax.all_to_all(spread, GRP, 0, 0, tiled=True)  13.1 us
    all_to_all x1, blocking collectives, on_device(): mine = lax.all_to_all(spread, PLANE, 0, 0, tiled=True)  12.2 us
    pallas_call x1, Pallas kernels, on_device(): pl.pallas_call(front_kernel, name='front', out_shape=(near(HALF + PACKED,...  4.3 us
    ppermute x1, starting transfers between devices, on_device(): other = lax.ppermute(mine, 'c', SWAP)  4.03 us
    pallas_call x1, Pallas kernels, on_device(): pl.pallas_call(update_kernel, name='update', compiler_params=LIMIT, out_s...  3.1 us
    pallas_call x2, Pallas kernels, finish(): pl.pallas_call(finish_kernel, name=name, compiler_params=LIMIT, grid=(1,)...  1.96 us
    pallas_call x1, Pallas kernels, on_device(): pl.pallas_call(keep_kernel, name='keep', compiler_params=LIMIT, out_shape...  1.68 us
  transfers between devices with their start and end apart: 2, of which 1 were waited for; matrix products, arithmetic and copies ran while one was open for 0% of the time, Pallas kernels for 4%

profile of v11, /device:TPU:1, one launch (start us, length us, event | category | flops | bytes accessed | tf_op | source)
XLA Modules:
  0.0 63.7 jit_solution(2321385909367895340)
XLA Ops:
  0.6 4.3 %front.1 = (f32[1064,128]{1,0:T(8,128)S(1)}, bf16[2048,256]{1,0:T(8,128)(2,1)S(1)}, f32[128,256]{1,0:T(8,128)S(1)}, f32[64,128]{1,0:T(8,128)S(1)}, f32[64,128]{1,0:T(8,128)S(1)}) custom-call(s32[2,128]{1,0:T(2,128)} %picks_hbm.1, s32[512]{0:T(512)} %ids_hbm.1, s32[8]{0:T(128)} %sweeps_hbm.1, bf16[2000,512]{1,0:T(8,128)(2,1)} %x_hbm.1, f32[64,2000]{1,0:T(8,128)} %w_hbm.1, ...), custom_call_target="tpu_custom_call" | custom-call | tf_op jit(solution)/shard_map/front/pallas_call | solution.py:416
  4.9 1.5 %collective-permute-start = (f32[1064,128]{1,0:T(8,128)S(1)}, f32[1064,128]{1,0:T(8,128)S(1)}, u32[]{:S(2)}, u32[]{:S(2)}) collective-permute-start(f32[1064,128]{1,0:T(8,128)S(1)} %get-tuple-element.19.send), channel_id=1, source_target_pairs={{0,1},{1,0},{2,3},{3,2},{4,5},{5,4},{6,7},{7,6},{8,9},{9,8},{10,11... | collective-permute-start | bytes 1634312 | tf_op jit(solution)/shard_map/ppermute | solution.py:440
  6.4 1.7 %keep.1 = (f32[1024,128]{1,0:T(8,128)S(1)}, f32[2,64,128]{2,1,0:T(8,128)}, bf16[256,8192]{1,0:T(8,128)(2,1)S(1)}) custom-call(bf16[2048,256]{1,0:T(8,128)(2,1)S(1)} %get-tuple-element.15.cells, f32[128,256]{1,0:T(8,128)S(1)} %get-tuple-element.16.state), custom_call_target="tpu_custom_call" | custom-call | tf_op jit(solution)/shard_map/keep/pallas_call | solution.py:441
  8.1 0.0 collective-permute-done.came
  8.1 0.1 pack.1
  8.2 20.3 %all_to_all.15.came = f32[8,168,128]{2,1,0:T(8,128)S(1)} all-to-all(f32[8,168,128]{2,1,0:T(8,128)S(1)} %pack.1), channel_id=1, replica_groups=mesh['y'=4,'xl'=2,'xh'=2,'z'=4,'c'=2] {'z','xh'}, dimensions={0} | all-to-all | bytes 1376256 | tf_op jit(solution)/shard_map/all_to_all | solution.py:457
  28.5 0.2 group.1
  28.7 13.1 %all_to_all.16.came = f32[8,136,128]{2,1,0:T(8,128)S(1)} all-to-all(f32[8,136,128]{2,1,0:T(8,128)S(1)} %group.1), channel_id=1, replica_groups=mesh['y'=4,'xl'=2,'xh'=2,'z'=4,'c'=2] {'xl','y'}, dimensions={0} | all-to-all | bytes 1114112 | tf_op jit(solution)/shard_map/all_to_all | solution.py:461
  41.8 3.1 %update.1 = f32[16,64,128]{2,1,0:T(8,128)S(1)} custom-call(f32[8,136,128]{2,1,0:T(8,128)S(1)} %all_to_all.16.came, f32[64,128]{1,0:T(8,128)S(1)} %get-tuple-element.21.w_own, bf16[256,8192]{1,0:T(8,128)(2,1)S(1)} %get-tuple-element.22.spread), custom_call_target="tpu_custom_call" | custom-call | tf_op jit(solution)/shard_map/update/pallas_call | solution.py:462
  44.9 12.2 %all_to_all.17.part = f32[16,64,128]{2,1,0:T(8,128)S(1)} all-to-all(f32[16,64,128]{2,1,0:T(8,128)S(1)} %update.1), channel_id=1, replica_groups=mesh['y'=4,'xl'=2,'xh'=2,'z'=4,'c'=2] {'xh','xl','z'}, dimensions={0} | all-to-all | bytes 1048576 | tf_op jit(solution)/shard_map/all_to_all | solution.py:473
  57.1 4.0 %collective-permute-start.1 = (f32[16,64,128]{2,1,0:T(8,128)S(1)}, f32[16,64,128]{2,1,0:T(8,128)S(1)}, u32[]{:S(2)}, u32[]{:S(2)}) collective-permute-start(f32[16,64,128]{2,1,0:T(8,128)S(1)} %all_to_all.17.part), channel_id=1, source_target_pairs={{0,1},{1,0},{2,3},{3,2},{4,5},{5,4},{6,7},{7,6},{8,9},{9,8},{10,11... | collective-permute-start | bytes 1572872 | tf_op jit(solution)/shard_map/ppermute | solution.py:474
  61.1 1.0 %mine.1 = (f32[64,2000]{1,0:T(8,128)}, f32[1,64,2000]{2,1,0:T(8,128)}) custom-call(f32[16,64,128]{2,1,0:T(8,128)S(1)} %all_to_all.17.part), custom_call_target="tpu_custom_call" | custom-call | tf_op jit(solution)/shard_map/mine/pallas_call | solution.py:382
  62.1 0.6 collective-permute-done.1.part
  62.7 1.0 %other.1 = (f32[64,2000]{1,0:T(8,128)}, f32[1,64,2000]{2,1,0:T(8,128)}) custom-call(f32[16,64,128]{2,1,0:T(8,128)S(1)} %collective-permute-done.1.part, f32[64,2000]{1,0:T(8,128)} %get-tuple-element.23.refs_0_, f32[1,64,2000]{2,1,0:T(8,128)} %get-tuple-element.24.refs_1_), custom_call_target="tpu_custom_call", output_to_operand_aliasing={{0}: (1, {}), {1}: (2, {})} | custom-call | tf_op jit(solution)/shard_map/other/pallas_call | solution.py:382
Async XLA Ops:
  4.9 3.1 %collective-permute-start = (f32[1064,128]{1,0:T(8,128)S(1)}, f32[1064,128]{1,0:T(8,128)S(1)}, u32[]{:S(2)}, u32[]{:S(2)}) collective-permute-start(f32[1064,128]{1,0:T(8,128)S(1)} %get-tuple-element.19.send), channel_id=1, source_target_pairs={{0,1},{1,0},{2,3},{3,2},{4,5},{5,4},{6,7},{7,6},{8,9},{9,8},{10,11... | collective-permute-start | bytes 1634312 | tf_op jit(solution)/shard_map/ppermute | solution.py:440
  57.1 5.6 %collective-permute-start.1 = (f32[16,64,128]{2,1,0:T(8,128)S(1)}, f32[16,64,128]{2,1,0:T(8,128)S(1)}, u32[]{:S(2)}, u32[]{:S(2)}) collective-permute-start(f32[16,64,128]{2,1,0:T(8,128)S(1)} %all_to_all.17.part), channel_id=1, source_target_pairs={{0,1},{1,0},{2,3},{3,2},{4,5},{5,4},{6,7},{7,6},{8,9},{9,8},{10,11... | collective-permute-start | bytes 1572872 | tf_op jit(solution)/shard_map/ppermute | solution.py:474
